TPU v7x, 256 devices: a whole 4x4x8 slice. The times are simulated.
256 devices in a mesh: gy: 16 (over z, y_lo), gz: 16 (over y_hi, x, core).
Axes of the slice: x: 4, y: 4 (y_hi: 2, y_lo: 2; y = y_hi * 2 + y_lo), z: 8, core: 2. Of those that a mesh axis runs over, the one named last changes fastest.
Arguments:
- velocity: float32 [3, 128, 128, 512], P(None, 'gy', 'gz'), may hold values from -6 to 6
- forcing: float32 [3, 128, 128, 512], P(None, 'gy', 'gz'), may hold values from -1.5 to 1.5, as said below
- first_kernel: bfloat16 [16, 3, 3, 3, 3], replicated, may hold values from -0.625 to 0.625
- first_bias: float32 [16], replicated, may hold values from -3 to 3
- second_kernel: bfloat16 [9, 16, 3, 3, 3], replicated, may hold values from -0.3125 to 0.3125
Outputs:
- velocity_next: float32 [3, 128, 128, 512], P(None, 'gy', 'gz')
Inputs may be any that keep to these rules, and one draw needn't show every extreme that they name: forcing increment of one step.
All inputs are finite; a program needn't handle non-finite values.
Results may differ from a plain program's by a relative error of at most 0.0028.
Values may be sent and summed in bfloat16 or wider, within the bound.
A program may use at most 64 MiB of HBM per device.

v0:
```python
from functools import reduce
import math

import jax
import jax.numpy as jnp
from jax import lax
from jax.sharding import PartitionSpec as P

time_step = 0.02
viscosity = 0.002
highest = lax.Precision.HIGHEST


def extended_2(block, sides, width):
    for axis, dim in sides:
        count = lax.axis_size(axis)
        forward = [(i, i + 1) for i in range(count - 1)]
        forward.append((count - 1, 0))
        backward = [(target, source) for source, target in forward]
        low = lax.ppermute(
            lax.slice_in_dim(block, block.shape[dim] - width, None, axis=dim), axis, forward
        )
        high = lax.ppermute(lax.slice_in_dim(block, 0, width, axis=dim), axis, backward)
        block = jnp.concatenate([low, block, high], axis=dim)
    return block


def signed_modes(offset, number, extent):
    raw_modes = offset + jnp.arange(number, dtype=jnp.int32)
    waves = jnp.where(2 * raw_modes > extent, raw_modes - extent, raw_modes)
    waves = jnp.where(2 * raw_modes == extent, 0, waves)
    return waves.astype(jnp.float32)


def fourier_tables(extent):
    indices = jnp.arange(extent, dtype=jnp.int32)
    phases = indices[:, None] * indices[None, :] % extent
    angles = phases.astype(jnp.float32) * (2.0 * math.pi / extent)
    return (jnp.cos(angles), jnp.sin(angles))


def contract(pattern, values, matrix):
    return jnp.einsum(pattern, values, matrix, precision=highest)


def periodic_convolution(source, weight):
    channels = source.shape[0]
    inner_rows = source.shape[1] - 2
    inner_depth = source.shape[2] - 2
    stacked = jnp.concatenate([jnp.roll(source, 1 - offset, axis=3) for offset in range(3)], axis=0)
    matrices = jnp.transpose(weight, (0, 2, 3, 4, 1)).reshape(weight.shape[0], 3, 3, 3 * channels)
    partial_sums = []
    for first_shift in range(3):
        for second_shift in range(3):
            window = stacked[
                :,
                first_shift : first_shift + inner_rows,
                second_shift : second_shift + inner_depth,
                :,
            ]
            partial_sums.append(
                jnp.einsum(
                    "ok,kyzx->oyzx",
                    matrices[:, first_shift, second_shift],
                    window,
                    preferred_element_type=jnp.float32,
                )
            )
    return reduce(jnp.add, partial_sums)


def tendency(extended, learned_first, learned_rest, spacings):
    center = extended[:, 1:-1, 1:-1]
    flux_first = center * center[0:1] + learned_first
    divergence = (jnp.roll(flux_first, -1, axis=3) - jnp.roll(flux_first, 1, axis=3)) / (
        2.0 * spacings[0]
    )
    column = extended[:, :, 1:-1]
    flux_second = column * column[1:2] + learned_rest[:, 0, :, 1:-1]
    divergence = divergence + (flux_second[:, 2:] - flux_second[:, :-2]) / (2.0 * spacings[1])
    planes = extended[:, 1:-1, :]
    flux_third = planes * planes[2:3] + learned_rest[:, 1, 1:-1, :]
    divergence = divergence + (flux_third[:, :, 2:] - flux_third[:, :, :-2]) / (2.0 * spacings[2])
    laplacian = (
        jnp.roll(center, -1, axis=3) + jnp.roll(center, 1, axis=3) - 2.0 * center
    ) / spacings[0] ** 2
    laplacian = (
        laplacian
        + (extended[:, 2:, 1:-1] + extended[:, :-2, 1:-1] - 2.0 * center) / spacings[1] ** 2
    )
    laplacian = (
        laplacian
        + (extended[:, 1:-1, 2:] + extended[:, 1:-1, :-2] - 2.0 * center) / spacings[2] ** 2
    )
    return viscosity * laplacian - divergence


def body(velocity, forcing, first_kernel, first_bias, second_kernel):
    row_devices = lax.axis_size("gy")
    depth_devices = lax.axis_size("gz")
    local_rows = velocity.shape[1]
    local_depth = velocity.shape[2]
    line_cells = velocity.shape[3]
    all_rows = local_rows * row_devices
    all_depth = local_depth * depth_devices
    line_block = line_cells // row_devices
    row_block = all_rows // depth_devices
    merged = local_depth * line_block
    spacings = (2.0 * math.pi / line_cells, 2.0 * math.pi / all_rows, 2.0 * math.pi / all_depth)
    bias_column = first_bias[:, None, None, None]
    extended = extended_2(velocity, (("gy", 1), ("gz", 2)), 1)
    hidden = jax.nn.silu(
        periodic_convolution(extended.astype(jnp.bfloat16), first_kernel) + bias_column
    ).astype(jnp.bfloat16)
    hidden_wide = extended_2(hidden, (("gy", 1), ("gz", 2)), 1)
    correction = periodic_convolution(hidden_wide, second_kernel).astype(jnp.bfloat16)
    correction = correction.reshape(3, 3, local_rows, local_depth, line_cells)
    learned_first = correction[:, 0]
    learned_rest = extended_2(correction[:, 1:], (("gy", 2), ("gz", 3)), 1)
    stepped = (
        velocity + time_step * tendency(extended, learned_first, learned_rest, spacings) + forcing
    )
    cosine_lines, sine_lines = fourier_tables(line_cells)
    cosine_rows, sine_rows = fourier_tables(all_rows)
    cosine_depth, sine_depth = fourier_tables(all_depth)
    row_index = lax.axis_index("gy")
    depth_index = lax.axis_index("gz")
    forward_cosine_lines = cosine_lines.reshape(line_cells, row_devices, line_block)
    forward_sine_lines = sine_lines.reshape(line_cells, row_devices, line_block)
    real_lines = contract("cyzx,xgk->cygzk", stepped, forward_cosine_lines).reshape(
        3, local_rows, row_devices, merged
    )
    imag_lines = -contract("cyzx,xgk->cygzk", stepped, forward_sine_lines).reshape(
        3, local_rows, row_devices, merged
    )
    spectrum = jnp.stack([real_lines, imag_lines])
    forward_cosine_rows = cosine_rows.reshape(all_rows, depth_devices, row_block)
    forward_sine_rows = sine_rows.reshape(all_rows, depth_devices, row_block)
    pieces = lax.all_to_all(spectrum, "gy", split_axis=3, concat_axis=2, tiled=True)
    real_part = pieces[0][:, :, 0]
    imag_part = pieces[1][:, :, 0]
    new_real = contract("cym,yhb->chbm", real_part, forward_cosine_rows) + contract(
        "cym,yhb->chbm", imag_part, forward_sine_rows
    )
    new_imag = contract("cym,yhb->chbm", imag_part, forward_cosine_rows) - contract(
        "cym,yhb->chbm", real_part, forward_sine_rows
    )
    row_spectrum = jnp.stack([new_real, new_imag])
    depth_spectrum = lax.all_to_all(row_spectrum, "gz", split_axis=2, concat_axis=2, tiled=True)
    real_input = depth_spectrum[0].reshape(3, depth_devices, row_block, local_depth, line_block)
    imag_input = depth_spectrum[1].reshape(3, depth_devices, row_block, local_depth, line_block)
    forward_cosine_depth = cosine_depth.reshape(depth_devices, local_depth, all_depth)
    forward_sine_depth = sine_depth.reshape(depth_devices, local_depth, all_depth)
    real_modes = contract("cgbzk,gzq->cbkq", real_input, forward_cosine_depth) + contract(
        "cgbzk,gzq->cbkq", imag_input, forward_sine_depth
    )
    imag_modes = contract("cgbzk,gzq->cbkq", imag_input, forward_cosine_depth) - contract(
        "cgbzk,gzq->cbkq", real_input, forward_sine_depth
    )
    line_waves = signed_modes(row_index * line_block, line_block, line_cells)[None, :, None]
    row_waves = signed_modes(depth_index * row_block, row_block, all_rows)[:, None, None]
    depth_waves = signed_modes(0, all_depth, all_depth)[None, None, :]
    squared = line_waves**2 + row_waves**2 + depth_waves**2
    inverse_square = jnp.where(squared > 0, 1.0 / jnp.maximum(squared, 1.0), 0.0)
    potential_real = (
        line_waves * real_modes[0] + row_waves * real_modes[1] + depth_waves * real_modes[2]
    ) * inverse_square
    potential_imag = (
        line_waves * imag_modes[0] + row_waves * imag_modes[1] + depth_waves * imag_modes[2]
    ) * inverse_square
    back_cosine_depth = cosine_depth.reshape(all_depth, depth_devices, local_depth)
    back_sine_depth = sine_depth.reshape(all_depth, depth_devices, local_depth)
    wave_list = (line_waves, row_waves, depth_waves)
    projected_real = jnp.stack(
        [real_modes[component] - wave_list[component] * potential_real for component in range(3)]
    )
    projected_imag = jnp.stack(
        [imag_modes[component] - wave_list[component] * potential_imag for component in range(3)]
    )
    item_count = projected_real.shape[0]
    result_real = contract("cbkq,qgz->cgbzk", projected_real, back_cosine_depth) - contract(
        "cbkq,qgz->cgbzk", projected_imag, back_sine_depth
    )
    result_imag = contract("cbkq,qgz->cgbzk", projected_real, back_sine_depth) + contract(
        "cbkq,qgz->cgbzk", projected_imag, back_cosine_depth
    )
    leaving = jnp.stack(
        [
            result_real.reshape(item_count, depth_devices, row_block, merged),
            result_imag.reshape(item_count, depth_devices, row_block, merged),
        ]
    )
    returned = lax.all_to_all(leaving, "gz", split_axis=2, concat_axis=2, tiled=True)
    returned = returned.reshape(2, returned.shape[1], all_rows, merged)
    back_cosine_rows = cosine_rows.reshape(all_rows, row_devices, local_rows)
    back_sine_rows = sine_rows.reshape(all_rows, row_devices, local_rows)
    real_field = returned[0]
    imag_field = returned[1]
    result_real = contract("cym,ygb->cgbm", real_field, back_cosine_rows) - contract(
        "cym,ygb->cgbm", imag_field, back_sine_rows
    )
    result_imag = contract("cym,ygb->cgbm", real_field, back_sine_rows) + contract(
        "cym,ygb->cgbm", imag_field, back_cosine_rows
    )
    leaving_lines = jnp.stack([result_real, result_imag])
    back_cosine_lines = cosine_lines.reshape(row_devices, line_block, line_cells)
    back_sine_lines = sine_lines.reshape(row_devices, line_block, line_cells)
    norm_factor = 1.0 / (line_cells * all_rows * all_depth)
    pieces = lax.all_to_all(leaving_lines, "gy", split_axis=2, concat_axis=2, tiled=True)
    item_count = pieces.shape[1]
    real_part = pieces[0].reshape(item_count, row_devices, local_rows, local_depth, line_block)
    imag_part = pieces[1].reshape(item_count, row_devices, local_rows, local_depth, line_block)
    physical_part = contract("cgyzk,gkx->cyzx", real_part, back_cosine_lines) - contract(
        "cgyzk,gkx->cyzx", imag_part, back_sine_lines
    )
    return physical_part * norm_factor


def solution(mesh):
    placed = (P(None, "gy", "gz", None), P(None, "gy", "gz", None), P(), P(), P())
    return jax.shard_map(
        body, mesh=mesh, in_specs=placed, out_specs=P(None, "gy", "gz", None), check_vma=False
    )
```

profile of v0, /device:TPU:1, one launch (start us, length us, event | category | flops | bytes accessed | tf_op | source)
XLA Modules:
  0.0 235.0 jit_solution(17750827669358431545)
XLA Ops:
  0.9 2.2 collective-permute-start.1
  3.1 5.4 %collective-permute-start = (f32[3,1,8,512]{3,2,1,0:T(8,128)S(1)}, f32[3,1,8,512]{3,2,1,0:T(8,128)S(1)}, u32[]{:S(2)}, u32[]{:S(2)}) collective-permute-start(f32[3,1,8,512]{3,2,1,0:T(8,128)S(1)} %get-tuple-element.56), channel_id=1, source_target_pairs={{16,0},{32,16},{48,32},{64,48},{80,64},{96,80},{112,96},{128,112},... | collective-permute-start | bytes 147464 | tf_op jit(solution)/shard_map/ppermute | solution.py:23
  14.3 1.8 collective-permute-done.2
  16.1 2.0 collective-permute-done.3
  24.2 2.5 %fusion.3 = bf16[16,8,8,512]{3,0,2,1:T(8,128)(2,1)S(1)} fusion(f32[8,8,512,16]{2,3,1,0:T(8,128)S(1)} %fusion.24, f32[8,8,512,16]{2,3,1,0:T(8,128)S(1)} %fusion.26, f32[8,8,512,16]{2,3,1,0:T(8,128)S(1)} %fusion.28, f32[8,8,512,16]{2,3,1,0:T(8,128)S(1)} %fusion.30, f32[8,8,512,16]{2,3,1,0:T(8,128)S(1)} %fusion.32, f32[8,8,512,16]{2,3,1,0:T(8,128)S(1)} %fusion.34, ...), kind=kOutput, calls=%fused_computation.7 | convolution fusion | flops 16777216 | bytes 18415968 | tf_op jit(solution)/shard_map/ok,kyzx->oyzx/dot_general | solution.py:62
  26.7 9.1 %collective-permute-start.4 = (bf16[16,1,8,512]{3,0,2,1:T(8,128)(2,1)S(1)}, bf16[16,1,8,512]{3,0,2,1:T(8,128)(2,1)S(1)}, u32[]{:S(2)}, u32[]{:S(2)}) collective-permute-start(bf16[16,1,8,512]{3,0,2,1:T(8,128)(2,1)S(1)} %get-tuple-element.24), channel_id=1, source_target_pairs={{0,16},{16,32},{32,48},{48,64},{64,80},{80,96},{96,112},{112,128},... | collective-permute-start | bytes 393224 | tf_op jit(solution)/shard_map/ppermute | solution.py:20
  35.8 3.6 %collective-permute-start.5 = (bf16[16,1,8,512]{3,0,2,1:T(8,128)(2,1)S(1)}, bf16[16,1,8,512]{3,0,2,1:T(8,128)(2,1)S(1)}, u32[]{:S(2)}, u32[]{:S(2)}) collective-permute-start(bf16[16,1,8,512]{3,0,2,1:T(8,128)(2,1)S(1)} %get-tuple-element.25), channel_id=1, source_target_pairs={{16,0},{32,16},{48,32},{64,48},{80,64},{96,80},{112,96},{128,112},... | collective-permute-start | bytes 393224 | tf_op jit(solution)/shard_map/ppermute | solution.py:23
  39.6 2.2 collective-permute-done.4
  41.8 2.4 %collective-permute-start.6 = (bf16[16,10,1,512]{3,0,2,1:T(8,128)(2,1)S(1)}, bf16[16,10,1,512]{3,0,2,1:T(8,128)(2,1)S(1)}, u32[]{:S(2)}, u32[]{:S(2)}) collective-permute-start(bf16[16,10,1,512]{3,0,2,1:T(8,128)(2,1)S(1)} %get-tuple-element.22), channel_id=1, source_target_pairs={{0,1},{1,2},{2,3},{3,4},{4,5},{5,6},{6,7},{7,8},{8,9},{9,10},{10,1... | collective-permute-start | bytes 491528 | tf_op jit(solution)/shard_map/ppermute | solution.py:20
  44.1 5.5 %collective-permute-start.7 = (bf16[16,10,1,512]{3,0,2,1:T(8,128)(2,1)S(1)}, bf16[16,10,1,512]{3,0,2,1:T(8,128)(2,1)S(1)}, u32[]{:S(2)}, u32[]{:S(2)}) collective-permute-start(bf16[16,10,1,512]{3,0,2,1:T(8,128)(2,1)S(1)} %get-tuple-element.23), channel_id=1, source_target_pairs={{1,0},{2,1},{3,2},{4,3},{5,4},{6,5},{7,6},{8,7},{9,8},{10,9},{11,1... | collective-permute-start | bytes 491528 | tf_op jit(solution)/shard_map/ppermute | solution.py:23
  52.1 3.1 %maximum_maximum_fusion = bf16[48,10,10,512]{3,0,2,1:T(8,128)(2,1)S(1)} fusion(bf16[16,10,10,1]{3,0,2,1:T(8,128)(2,1)S(1)} %get-tuple-element.10, bf16[16,10,10,511]{3,0,2,1:T(8,128)(2,1)S(1)} %get-tuple-element.12, bf16[16,10,1,512]{3,0,2,1:T(8,128)(2,1)S(1)} %collective-permute-done.7, bf16[16,1,8,512]{3,0,2,1:T(8,128)(2,1)S(1)} %collective-permute-done.5, ...), kind=kLoop, calls=%fused_computation | loop fusion | flops 44236800 | bytes 9830400 | tf_op jit(solution)/shard_map/concatenate | solution.py:50
  59.8 2.1 fusion.4
  63.2 3.9 %collective-permute-start.9 = (bf16[3,2,1,8,512]{4,3,2,0,1:T(8,128)(2,1)S(1)}, bf16[3,2,1,8,512]{4,3,2,0,1:T(8,128)(2,1)S(1)}, u32[]{:S(2)}, u32[]{:S(2)}) collective-permute-start(bf16[3,2,1,8,512]{4,3,2,0,1:T(8,128)(2,1)S(1)} %copy.326), channel_id=1, source_target_pairs={{16,0},{32,16},{48,32},{64,48},{80,64},{96,80},{112,96},{128,112},... | collective-permute-start | bytes 147464 | tf_op jit(solution)/shard_map/ppermute | solution.py:23
  68.5 8.2 %collective-permute-start.11 = (bf16[3,2,10,1,512]{4,3,2,0,1:T(2,128)(2,1)S(1)}, bf16[3,2,10,1,512]{4,3,2,0,1:T(2,128)(2,1)S(1)}, u32[]{:S(2)}, u32[]{:S(2)}) collective-permute-start(bf16[3,2,10,1,512]{4,3,2,0,1:T(2,128)(2,1)S(1)} %get-tuple-element.41), channel_id=1, source_target_pairs={{1,0},{2,1},{3,2},{4,3},{5,4},{6,5},{7,6},{8,7},{9,8},{10,9},{11,1... | collective-permute-start | bytes 184328 | tf_op jit(solution)/shard_map/ppermute | solution.py:23
  78.6 6.7 %convolution_bitcast_fusion = f32[3,8,16,8,32]{4,3,1,0,2:T(8,128)S(1)} fusion(f32[3,8,8,512,1]{3,2,1,0,4:T(8,128)S(1)} %fusion.61, s32[16,32]{1,0:T(8,128)S(1)} %multiply_add_fusion), kind=kOutput, calls=%fused_computation.18 | convolution fusion | flops 607649792 | bytes 788480 | tf_op jit(solution)/shard_map/cyzx,xgk->cygzk/dot_general | solution.py:43
  85.4 6.8 %negate_bitcast_fusion = f32[3,8,16,8,32]{4,3,1,0,2:T(8,128)S(1)} fusion(f32[3,8,8,512,1]{3,2,1,0,4:T(8,128)S(1)} %fusion.61, s32[16,32]{1,0:T(8,128)S(1)} %multiply_add_fusion), kind=kOutput, calls=%fused_computation.14 | convolution fusion | flops 607748096 | bytes 788480 | tf_op jit(solution)/shard_map/cyzx,xgk->cygzk/dot_general | solution.py:43
  94.0 7.3 %all-to-all-start = ((f32[2,3,8,16,256]{4,2,1,0,3:T(8,128)}), f32[2,3,8,16,256]{4,2,1,0,3:T(8,128)S(1)}, u32[]{:S(2)}, u32[]{:S(2)}) async-start(f32[2,3,8,16,256]{4,2,1,0,3:T(8,128)} %pad_maximum_fusion.2), calls=%async_computation | async-start | bytes 1572864 | tf_op jit(solution)/shard_map/all_to_all | solution.py:139
  101.3 14.6 %all-to-all-done = f32[2,3,8,16,256]{4,2,1,0,3:T(8,128)S(1)} async-done(((f32[2,3,8,16,256]{4,2,1,0,3:T(8,128)}), f32[2,3,8,16,256]{4,2,1,0,3:T(8,128)S(1)}, u32[]{:S(2)}, u32[]{:S(2)}) %all-to-all-start) | async-done | bytes 786464 | tf_op jit(solution)/shard_map/all_to_all | solution.py:139
  120.1 17.4 %all-to-all-start.1 = ((f32[2,3,16,8,256]{4,3,1,0,2:T(8,128)}), f32[2,3,16,8,256]{4,3,1,0,2:T(8,128)S(1)}, u32[]{:S(2)}, u32[]{:S(2)}) async-start(f32[2,3,16,8,256]{4,3,1,0,2:T(8,128)} %copy.246), calls=%async_computation.1 | async-start | bytes 1572864 | tf_op jit(solution)/shard_map/all_to_all | solution.py:149
  139.3 12.5 %all-to-all-done.1 = f32[2,3,16,8,256]{4,3,1,0,2:T(8,128)S(1)} async-done(((f32[2,3,16,8,256]{4,3,1,0,2:T(8,128)}), f32[2,3,16,8,256]{4,3,1,0,2:T(8,128)S(1)}, u32[]{:S(2)}, u32[]{:S(2)}) %all-to-all-start.1) | async-done | bytes 786464 | tf_op jit(solution)/shard_map/all_to_all | solution.py:149
  152.2 3.5 %convolution_bitcast_fusion.5 = f32[3,8,32,128]{3,2,1,0:T(8,128)} fusion(f32[3,16,8,8,32]{4,3,2,0,1:T(8,128)S(1)} %reshape.497, s32[16,8]{1,0:T(8,128)S(1)} %multiply_add_fusion.1), kind=kOutput, calls=%fused_computation.25 | convolution fusion | flops 151224320 | bytes 786944 | tf_op jit(solution)/shard_map/cgbzk,gzq->cbkq/dot_general | solution.py:43
  156.1 2.7 %convolution_bitcast_fusion.3 = f32[3,8,32,128]{3,2,1,0:T(8,128)S(1)} fusion(f32[3,16,8,8,32]{4,3,2,0,1:T(8,128)S(1)} %reshape.496, s32[16,8]{1,0:T(8,128)S(1)} %multiply_add_fusion.1), kind=kOutput, calls=%fused_computation.23 | convolution fusion | flops 151224320 | bytes 786944 | tf_op jit(solution)/shard_map/cgbzk,gzq->cbkq/dot_general | solution.py:43
  158.8 2.7 %fusion.11 = f32[3,8,32,128]{3,2,1,0:T(8,128)S(1)} fusion(f32[3,8,32,128]{3,2,1,0:T(8,128)S(1)} %copy-done.13, f32[3,16,8,8,32]{4,3,2,0,1:T(8,128)S(1)} %reshape.496, s32[16,8]{1,0:T(8,128)S(1)} %multiply_add_fusion.1), kind=kOutput, calls=%fused_computation.37 | convolution fusion | flops 151322624 | bytes 1180160 | tf_op jit(solution)/shard_map/cgbzk,gzq->cbkq/dot_general | solution.py:43
  161.6 2.7 %fusion.12 = f32[3,8,32,128]{3,2,1,0:T(8,128)S(1)} fusion(f32[3,8,32,128]{3,2,1,0:T(8,128)S(1)} %convolution_bitcast_fusion.3, f32[3,16,8,8,32]{4,3,2,0,1:T(8,128)S(1)} %reshape.497, s32[16,8]{1,0:T(8,128)S(1)} %multiply_add_fusion.1), kind=kOutput, calls=%fused_computation.38 | convolution fusion | flops 151322624 | bytes 1180160 | tf_op jit(solution)/shard_map/cgbzk,gzq->cbkq/dot_general | solution.py:43
  164.7 2.2 fusion.97
  166.9 2.6 %fusion.96 = f32[16,8,3,8,32]{4,1,3,2,0:T(8,128)S(1)} fusion(f32[1,8,32,128]{3,2,1,0:T(8,128)S(1)} %get-tuple-element.39, f32[1,8,32,128]{3,2,1,0:T(8,128)S(1)} %get-tuple-element.38, f32[1,8,32,128]{3,2,1,0:T(8,128)S(1)} %get-tuple-element.76, s32[16,8]{1,0:T(8,128)S(1)} %multiply_add_fusion.1), kind=kOutput, calls=%fused_computation.140 | convolution fusion | flops 151420928 | bytes 786944 | tf_op jit(solution)/shard_map/cbkq,qgz->cgbzk/dot_general | solution.py:43
  169.5 2.2 subtract_bitcast_fusion
  172.2 3.2 %add_bitcast_fusion = f32[3,16,8,8,32]{4,3,2,0,1:T(8,128)S(1)} fusion(f32[16,8,3,8,32]{4,1,3,2,0:T(8,128)S(1)} %fusion.96, f32[1,8,32,128]{3,2,1,0:T(8,128)} %copy-done.2, f32[1,8,32,128]{3,2,1,0:T(8,128)} %copy-done.3, f32[1,8,32,128]{3,2,1,0:T(8,128)} %copy-done.1, s32[16,8]{1,0:T(8,128)S(1)} %multiply_add_fusion.1), kind=kOutput, calls=%fused_computation.12 | convolution fusion | flops 151519232 | bytes 1180160 | tf_op jit(solution)/shard_map/cbkq,qgz->cgbzk/dot_general | solution.py:43
  175.9 17.8 %all_to_all.30 = f32[2,3,16,8,256]{4,3,1,0,2:T(8,128)S(1)} all-to-all(f32[2,3,16,8,256]{4,3,1,0,2:T(8,128)S(1)} %pad_maximum_fusion.4), channel_id=1, replica_groups=mesh['gy'=16,'gz'=16] {'gz'}, dimensions={2} | all-to-all | bytes 1572864 | tf_op jit(solution)/shard_map/all_to_all | solution.py:193
  197.1 24.8 %all_to_all.31 = f32[2,3,16,8,256]{4,3,1,0,2:T(8,128)S(1)} all-to-all(f32[2,3,16,8,256]{4,3,1,0,2:T(8,128)S(1)} %copy.257), channel_id=1, replica_groups=mesh['gy'=16,'gz'=16] {'gy'}, dimensions={2} | all-to-all | bytes 1572864 | tf_op jit(solution)/shard_map/all_to_all | solution.py:209
  222.6 5.5 %convolution_bitcast_fusion.1 = f32[3,8,8,512]{3,2,1,0:T(8,128)S(1)} fusion(f32[3,16,8,8,32]{4,3,2,0,1:T(8,128)S(1)} %reshape.495, s32[16,32]{1,0:T(8,128)S(1)} %copy-done.8), kind=kOutput, calls=%fused_computation.21 | convolution fusion | flops 607649792 | bytes 788480 | tf_op jit(solution)/shard_map/cgyzk,gkx->cyzx/dot_general | solution.py:43
  228.5 6.3 %fusion.10 = f32[3,8,8,512]{3,2,1,0:T(8,128)} fusion(f32[3,8,8,512]{3,2,1,0:T(8,128)S(1)} %convolution_bitcast_fusion.1, f32[3,16,8,8,32]{4,3,2,0,1:T(8,128)S(1)} %reshape.494, s32[16,32]{1,0:T(8,128)S(1)} %copy-done.8), kind=kOutput, calls=%fused_computation.36 | convolution fusion | flops 607846400 | bytes 1181696 | tf_op jit(solution)/shard_map/cgyzk,gkx->cyzx/dot_general | solution.py:43
  (142 shorter events, 38.5 us)
Async XLA Ops:
  0.0 10.7 %copy-start = (f32[3,8,8,512]{3,2,1,0:T(8,128)S(1)}, f32[3,8,8,512]{3,2,1,0:T(8,128)}, u32[]{:S(2)}) copy-start(f32[3,8,8,512]{3,2,1,0:T(8,128)} %param.5) | copy-start | bytes 1179652
  0.0 10.8 %copy-start.6 = (bf16[16,3,3,3,3]{0,4,3,2,1:T(4,128)(2,1)S(1)}, bf16[16,3,3,3,3]{0,4,3,2,1:T(4,128)(2,1)}, u32[]{:S(2)}) copy-start(bf16[16,3,3,3,3]{0,4,3,2,1:T(4,128)(2,1)} %param.7) | copy-start | bytes 7780
  0.0 10.8 %copy-start.5 = (bf16[9,16,3,3,3]{1,4,3,2,0:T(4,128)(2,1)S(1)}, bf16[9,16,3,3,3]{1,4,3,2,0:T(4,128)(2,1)}, u32[]{:S(2)}) copy-start(bf16[9,16,3,3,3]{1,4,3,2,0:T(4,128)(2,1)} %param.9) | copy-start | bytes 23332
  0.9 11.0 %collective-permute-start.1 = (f32[3,1,8,512]{3,2,1,0:T(8,128)S(1)}, f32[3,1,8,512]{3,2,1,0:T(8,128)S(1)}, u32[]{:S(2)}, u32[]{:S(2)}) collective-permute-start(f32[3,1,8,512]{3,2,1,0:T(8,128)S(1)} %get-tuple-element.57), channel_id=1, source_target_pairs={{0,16},{16,32},{32,48},{48,64},{64,80},{80,96},{96,112},{112,128},... | collective-permute-start | bytes 147464 | tf_op jit(solution)/shard_map/ppermute | solution.py:20
  3.1 8.9 %collective-permute-start = (f32[3,1,8,512]{3,2,1,0:T(8,128)S(1)}, f32[3,1,8,512]{3,2,1,0:T(8,128)S(1)}, u32[]{:S(2)}, u32[]{:S(2)}) collective-permute-start(f32[3,1,8,512]{3,2,1,0:T(8,128)S(1)} %get-tuple-element.56), channel_id=1, source_target_pairs={{16,0},{32,16},{48,32},{64,48},{80,64},{96,80},{112,96},{128,112},... | collective-permute-start | bytes 147464 | tf_op jit(solution)/shard_map/ppermute | solution.py:23
  11.0 74.3 %copy-start.7 = (s32[16,32]{1,0:T(8,128)}, s32[16,32]{1,0:T(8,128)S(1)}, u32[]{:S(2)}) copy-start(s32[16,32]{1,0:T(8,128)S(1)} %multiply_add_fusion) | copy-start | bytes 6148
  12.0 4.0 %collective-permute-start.2 = (f32[3,10,1,512]{3,2,1,0:T(1,128)S(1)}, f32[3,10,1,512]{3,2,1,0:T(1,128)S(1)}, u32[]{:S(2)}, u32[]{:S(2)}) collective-permute-start(f32[3,10,1,512]{3,2,1,0:T(1,128)S(1)} %get-tuple-element.47), channel_id=1, source_target_pairs={{1,0},{2,1},{3,2},{4,3},{5,4},{6,5},{7,6},{8,7},{9,8},{10,9},{11,1... | collective-permute-start | bytes 184328 | tf_op jit(solution)/shard_map/ppermute | solution.py:23
  13.1 5.0 %collective-permute-start.3 = (f32[3,10,1,512]{3,2,1,0:T(1,128)S(1)}, f32[3,10,1,512]{3,2,1,0:T(1,128)S(1)}, u32[]{:S(2)}, u32[]{:S(2)}) collective-permute-start(f32[3,10,1,512]{3,2,1,0:T(1,128)S(1)} %get-tuple-element.46), channel_id=1, source_target_pairs={{0,1},{1,2},{2,3},{3,4},{4,5},{5,6},{6,7},{7,8},{8,9},{9,10},{10,1... | collective-permute-start | bytes 184328 | tf_op jit(solution)/shard_map/ppermute | solution.py:20
  23.5 0.7 copy-start.12
  26.7 15.0 %collective-permute-start.4 = (bf16[16,1,8,512]{3,0,2,1:T(8,128)(2,1)S(1)}, bf16[16,1,8,512]{3,0,2,1:T(8,128)(2,1)S(1)}, u32[]{:S(2)}, u32[]{:S(2)}) collective-permute-start(bf16[16,1,8,512]{3,0,2,1:T(8,128)(2,1)S(1)} %get-tuple-element.24), channel_id=1, source_target_pairs={{0,16},{16,32},{32,48},{48,64},{64,80},{80,96},{96,112},{112,128},... | collective-permute-start | bytes 393224 | tf_op jit(solution)/shard_map/ppermute | solution.py:20
  35.8 5.9 %collective-permute-start.5 = (bf16[16,1,8,512]{3,0,2,1:T(8,128)(2,1)S(1)}, bf16[16,1,8,512]{3,0,2,1:T(8,128)(2,1)S(1)}, u32[]{:S(2)}, u32[]{:S(2)}) collective-permute-start(bf16[16,1,8,512]{3,0,2,1:T(8,128)(2,1)S(1)} %get-tuple-element.25), channel_id=1, source_target_pairs={{16,0},{32,16},{48,32},{64,48},{80,64},{96,80},{112,96},{128,112},... | collective-permute-start | bytes 393224 | tf_op jit(solution)/shard_map/ppermute | solution.py:23
  41.8 8.6 %collective-permute-start.6 = (bf16[16,10,1,512]{3,0,2,1:T(8,128)(2,1)S(1)}, bf16[16,10,1,512]{3,0,2,1:T(8,128)(2,1)S(1)}, u32[]{:S(2)}, u32[]{:S(2)}) collective-permute-start(bf16[16,10,1,512]{3,0,2,1:T(8,128)(2,1)S(1)} %get-tuple-element.22), channel_id=1, source_target_pairs={{0,1},{1,2},{2,3},{3,4},{4,5},{5,6},{6,7},{7,8},{8,9},{9,10},{10,1... | collective-permute-start | bytes 491528 | tf_op jit(solution)/shard_map/ppermute | solution.py:20
  44.1 6.5 %collective-permute-start.7 = (bf16[16,10,1,512]{3,0,2,1:T(8,128)(2,1)S(1)}, bf16[16,10,1,512]{3,0,2,1:T(8,128)(2,1)S(1)}, u32[]{:S(2)}, u32[]{:S(2)}) collective-permute-start(bf16[16,10,1,512]{3,0,2,1:T(8,128)(2,1)S(1)} %get-tuple-element.23), channel_id=1, source_target_pairs={{1,0},{2,1},{3,2},{4,3},{5,4},{6,5},{7,6},{8,7},{9,8},{10,9},{11,1... | collective-permute-start | bytes 491528 | tf_op jit(solution)/shard_map/ppermute | solution.py:23
  62.3 5.8 %collective-permute-start.8 = (bf16[3,2,1,8,512]{4,3,2,0,1:T(8,128)(2,1)S(1)}, bf16[3,2,1,8,512]{4,3,2,0,1:T(8,128)(2,1)S(1)}, u32[]{:S(2)}, u32[]{:S(2)}) collective-permute-start(bf16[3,2,1,8,512]{4,3,2,0,1:T(8,128)(2,1)S(1)} %copy.324), channel_id=1, source_target_pairs={{0,16},{16,32},{32,48},{48,64},{64,80},{80,96},{96,112},{112,128},... | collective-permute-start | bytes 147464 | tf_op jit(solution)/shard_map/ppermute | solution.py:20
  63.2 5.1 %collective-permute-start.9 = (bf16[3,2,1,8,512]{4,3,2,0,1:T(8,128)(2,1)S(1)}, bf16[3,2,1,8,512]{4,3,2,0,1:T(8,128)(2,1)S(1)}, u32[]{:S(2)}, u32[]{:S(2)}) collective-permute-start(bf16[3,2,1,8,512]{4,3,2,0,1:T(8,128)(2,1)S(1)} %copy.326), channel_id=1, source_target_pairs={{16,0},{32,16},{48,32},{64,48},{80,64},{96,80},{112,96},{128,112},... | collective-permute-start | bytes 147464 | tf_op jit(solution)/shard_map/ppermute | solution.py:23
  68.4 9.5 %copy-start.4 = (f32[3,8,8,512]{3,2,1,0:T(8,128)S(1)}, f32[3,8,8,512]{3,2,1,0:T(8,128)}, u32[]{:S(2)}) copy-start(f32[3,8,8,512]{3,2,1,0:T(8,128)} %param.6) | copy-start | bytes 1179652
  68.5 9.0 %collective-permute-start.10 = (bf16[3,2,10,1,512]{4,3,2,0,1:T(2,128)(2,1)S(1)}, bf16[3,2,10,1,512]{4,3,2,0,1:T(2,128)(2,1)S(1)}, u32[]{:S(2)}, u32[]{:S(2)}) collective-permute-start(bf16[3,2,10,1,512]{4,3,2,0,1:T(2,128)(2,1)S(1)} %get-tuple-element.40), channel_id=1, source_target_pairs={{0,1},{1,2},{2,3},{3,4},{4,5},{5,6},{6,7},{7,8},{8,9},{9,10},{10,1... | collective-permute-start | bytes 184328 | tf_op jit(solution)/shard_map/ppermute | solution.py:20
  68.5 9.2 %collective-permute-start.11 = (bf16[3,2,10,1,512]{4,3,2,0,1:T(2,128)(2,1)S(1)}, bf16[3,2,10,1,512]{4,3,2,0,1:T(2,128)(2,1)S(1)}, u32[]{:S(2)}, u32[]{:S(2)}) collective-permute-start(bf16[3,2,10,1,512]{4,3,2,0,1:T(2,128)(2,1)S(1)} %get-tuple-element.41), channel_id=1, source_target_pairs={{1,0},{2,1},{3,2},{4,3},{5,4},{6,5},{7,6},{8,7},{9,8},{10,9},{11,1... | collective-permute-start | bytes 184328 | tf_op jit(solution)/shard_map/ppermute | solution.py:23
  94.0 21.9 %all-to-all-start = ((f32[2,3,8,16,256]{4,2,1,0,3:T(8,128)}), f32[2,3,8,16,256]{4,2,1,0,3:T(8,128)S(1)}, u32[]{:S(2)}, u32[]{:S(2)}) async-start(f32[2,3,8,16,256]{4,2,1,0,3:T(8,128)} %pad_maximum_fusion.2), calls=%async_computation | async-start | bytes 1572864 | tf_op jit(solution)/shard_map/all_to_all | solution.py:139
  120.1 31.6 %all-to-all-start.1 = ((f32[2,3,16,8,256]{4,3,1,0,2:T(8,128)}), f32[2,3,16,8,256]{4,3,1,0,2:T(8,128)S(1)}, u32[]{:S(2)}, u32[]{:S(2)}) async-start(f32[2,3,16,8,256]{4,3,1,0,2:T(8,128)} %copy.246), calls=%async_computation.1 | async-start | bytes 1572864 | tf_op jit(solution)/shard_map/all_to_all | solution.py:149
  156.0 2.8 %copy-start.13 = (f32[3,8,32,128]{3,2,1,0:T(8,128)S(1)}, f32[3,8,32,128]{3,2,1,0:T(8,128)}, u32[]{:S(2)}) copy-start(f32[3,8,32,128]{3,2,1,0:T(8,128)} %convolution_bitcast_fusion.5) | copy-start | bytes 1179652
  161.6 2.8 %copy-start.9 = (f32[128]{0:T(128)S(1)}, f32[128]{0:T(128)}, u32[]{:S(2)}) copy-start(f32[128]{0:T(128)} %fusion.173) | copy-start | bytes 1540
  161.6 2.8 %copy-start.10 = (f32[32]{0:T(128)S(1)}, f32[32]{0:T(128)}, u32[]{:S(2)}) copy-start(f32[32]{0:T(128)} %fusion.174) | copy-start | bytes 388
  161.6 2.8 %copy-start.11 = (f32[128]{0:T(128)S(1)}, f32[128]{0:T(128)}, u32[]{:S(2)}) copy-start(f32[128]{0:T(128)} %fusion.176) | copy-start | bytes 1540
  164.6 4.9 %copy-start.1 = (f32[1,8,32,128]{3,2,1,0:T(8,128)}, f32[1,8,32,128]{3,2,1,0:T(8,128)S(1)}, u32[]{:S(2)}) copy-start(f32[1,8,32,128]{3,2,1,0:T(8,128)S(1)} %get-tuple-element.5) | copy-start | bytes 393220
  164.7 4.8 %copy-start.2 = (f32[1,8,32,128]{3,2,1,0:T(8,128)}, f32[1,8,32,128]{3,2,1,0:T(8,128)S(1)}, u32[]{:S(2)}) copy-start(f32[1,8,32,128]{3,2,1,0:T(8,128)S(1)} %get-tuple-element.78) | copy-start | bytes 393220
  164.7 4.8 %copy-start.3 = (f32[1,8,32,128]{3,2,1,0:T(8,128)}, f32[1,8,32,128]{3,2,1,0:T(8,128)S(1)}, u32[]{:S(2)}) copy-start(f32[1,8,32,128]{3,2,1,0:T(8,128)S(1)} %get-tuple-element.79) | copy-start | bytes 393220
  221.9 0.7 copy-start.8
where the time goes:
time: 240 us; the launch traced here: 235 us
  starting transfers between devices  67.5 us (28%)
  matrix products  66.6 us (28%)
  blocking collectives  42.6 us (18%)
  waiting for transfers between devices  36.1 us (15%)
  local copies, waits for them, and re-layouts  12.7 us (5%)
  other arithmetic  8.42 us (4%)
    dot_general x20, matrix products, contract(): return jnp.einsum(pattern, values, matrix, precision=highest)  53.4 us
    ppermute x6, starting transfers between devices, extended_2(): lax.ppermute(lax.slice_in_dim(block, 0, width, axis=dim), axis, backward)  27.6 us
    all_to_all x1, blocking collectives, body(): lax.all_to_all(leaving_lines, 'gy', split_axis=2, concat_axis=2, tiled=True)  24.8 us
    all_to_all x1, blocking collectives, body(): lax.all_to_all(leaving, 'gz', split_axis=2, concat_axis=2, tiled=True)  17.8 us
    all_to_all x1, starting transfers between devices, body(): lax.all_to_all(row_spectrum, 'gz', split_axis=2, concat_axis=2, tiled=True)  17.4 us
    ppermute x6, starting transfers between devices, extended_2(): lax.ppermute(lax.slice_in_dim(block, block.shape[dim] - width, None, axis...  15.4 us
    all_to_all x1, waiting for transfers between devices, body(): lax.all_to_all(spectrum, 'gy', split_axis=3, concat_axis=2, tiled=True)  14.6 us
    dot_general x18, matrix products, periodic_convolution(): jnp.einsum('ok,kyzx->oyzx', matrices[:, first_shift, second_shift], windo...  13.2 us
  transfers between devices with their start and end apart: 14, of which 11 were waited for; matrix products, arithmetic and copies ran while one was open for 2% of the time, Pallas kernels for 0%

commit v1 on v0

v1 whole, which is shorter than its diff:
```python
from functools import reduce
import math

import jax
import jax.numpy as jnp
import numpy as np
from jax import lax
from jax.experimental import pallas as pl
from jax.experimental.pallas import tpu as pltpu
from jax.sharding import PartitionSpec as P

time_step = 0.02
viscosity = 0.002
highest = lax.Precision.HIGHEST


def extended_2(block, sides, width):
    for axis, dim in sides:
        count = lax.axis_size(axis)
        forward = [(i, i + 1) for i in range(count - 1)]
        forward.append((count - 1, 0))
        backward = [(target, source) for source, target in forward]
        low = lax.ppermute(
            lax.slice_in_dim(block, block.shape[dim] - width, None, axis=dim), axis, forward
        )
        high = lax.ppermute(lax.slice_in_dim(block, 0, width, axis=dim), axis, backward)
        block = jnp.concatenate([low, block, high], axis=dim)
    return block


MESH = pl.DeviceIdType.MESH
BF = jnp.bfloat16
F32 = jnp.float32
GY, GZ = 16, 16
PEERS = GY * GZ
NL = 512
CELLS = 64


def halves(table):
    high = table.astype(BF)
    low = (table - high.astype(np.float64)).astype(BF)
    return high, low


def root_tables(size):
    index = np.arange(size)
    angle = 2.0 * np.pi * (np.outer(index, index) % size) / size
    return np.cos(angle), np.sin(angle)


def spectral_tables():
    mode = np.arange(PEERS)
    cell = np.arange(NL)
    angle = 2.0 * np.pi * (np.outer(mode, cell) % NL) / NL
    real, imag = np.cos(angle), -np.sin(angle)
    imag[0] = 1.0 - 2.0 * (cell % 2)
    lines = np.concatenate([real, imag], axis=0)
    cos16, sin16 = root_tables(16)
    wide_cos = np.kron(cos16, cos16) - np.kron(sin16, sin16)
    wide_sin = np.kron(sin16, cos16) + np.kron(cos16, sin16)
    outer = np.concatenate([wide_cos, wide_sin], axis=0)
    cos8, sin8 = root_tables(8)
    near_cos = np.kron(cos8, cos8) - np.kron(sin8, sin8)
    near_sin = np.kron(sin8, cos8) + np.kron(cos8, sin8)
    inner = np.block([[near_cos, -near_sin], [near_sin, near_cos]])
    row = np.arange(PEERS)
    lane = np.arange(2 * CELLS)
    first = np.outer(row // GZ, (lane % CELLS) // 8)
    second = np.outer(row % GZ, lane % 8)
    turn = 2.0 * np.pi * ((first + second) % 128) / 128
    sign = np.where(lane < CELLS, 1.0, -1.0)[None, :]
    twiddle = np.stack([np.cos(turn), np.sin(turn) * sign]).astype(np.float32)

    def signed(index):
        wave = np.where(2 * index > 128, index - 128, index)
        return np.where(2 * index == 128, 0, wave)

    wave_y = signed((row // GZ)[:, None] + 16 * ((lane % CELLS) // 8)[None, :])
    wave_z = signed((row % GZ)[:, None] + 16 * (lane % 8)[None, :])
    waves = np.stack([wave_y, wave_z]).astype(np.float32)
    return (*halves(lines), *halves(outer), *halves(inner), *halves(inner.T.copy()), twiddle, waves)


def split(value):
    high = value.astype(BF)
    return high, (value - high.astype(F32)).astype(BF)


def dot(left, right, dims=((1,), (0,))):
    return lax.dot_general(left, right, (dims, ((), ())), preferred_element_type=F32)


def enter(ready):
    gy, gz = lax.axis_index("gy"), lax.axis_index("gz")
    barrier = pltpu.get_barrier_semaphore()

    def greet(step, carry):
        pl.semaphore_signal(barrier, inc=1, device_id=(lax.rem(gy + step, GY), gz), device_id_type=MESH)
        pl.semaphore_signal(barrier, inc=1, device_id=(gy, lax.rem(gz + step, GZ)), device_id_type=MESH)
        return carry

    lax.fori_loop(1, 16, greet, 0)
    pl.semaphore_wait(barrier, GY + GZ - 2)

    def confirm(step, carry):
        pl.semaphore_signal(ready, inc=1, device_id=(gy, lax.rem(gz + step, GZ)), device_id_type=MESH)
        return carry

    lax.fori_loop(1, GZ, confirm, 0)
    pl.semaphore_wait(ready, GZ - 1)


def exchange(source, target, send_sem, recv_sem, own_sem):
    gy, gz = lax.axis_index("gy"), lax.axis_index("gz")
    me = gy * GZ + gz

    def send(step, carry):
        ty, tz = lax.rem(gy + lax.rem(step, GY), GY), lax.rem(gz + step // GY, GZ)
        pltpu.make_async_remote_copy(
            source.at[ty * GZ + tz],
            target.at[me],
            send_sem,
            recv_sem,
            device_id=(ty, tz),
            device_id_type=MESH,
        ).start()
        return carry

    lax.fori_loop(1, PEERS, send, 0)
    own = pltpu.make_async_copy(source.at[me], target.at[me], own_sem)
    own.start()
    own.wait()
    others = pl.ds(0, PEERS - 1)
    pltpu.make_async_copy(source.at[others], target.at[others], recv_sem).wait()
    pltpu.make_async_copy(source.at[others], target.at[others], send_sem).wait()


def pack(parts, staged, outgoing):
    rest = parts[0] - parts[0].astype(BF).astype(F32)
    for row, part in enumerate((*parts, rest)):
        staged[pl.ds(row, PEERS, stride=4), :] = part
    outgoing[...] = staged[...].astype(BF).reshape(PEERS, 4, 128)


def unpack(incoming, staged):
    staged[...] = incoming[...].astype(F32).reshape(PEERS * 4, 128)
    return [staged[pl.ds(row, PEERS, stride=4), :].astype(BF) for row in range(4)]


def swapped(value):
    return pltpu.roll(value, CELLS, axis=1)


def spectral(
    stepped,
    lines_high,
    lines_low,
    outer_high,
    outer_low,
    inner_high,
    inner_low,
    back_high,
    back_low,
    twiddle,
    waves,
    result,
    staged,
    outgoing,
    incoming,
    outgoing_back,
    incoming_back,
    sems,
    ready,
):
    enter(ready)
    gy, gz = lax.axis_index("gy"), lax.axis_index("gz")
    nt = ((1,), (1,))
    high, low = split(stepped[...].reshape(3 * CELLS, NL))
    modes = dot(lines_high[...], high, nt) + (dot(lines_low[...], high, nt) + dot(lines_high[...], low, nt))
    pack(
        [
            jnp.concatenate(
                [modes[:PEERS, CELLS * c : CELLS * (c + 1)], modes[PEERS:, CELLS * c : CELLS * (c + 1)]],
                axis=1,
            )
            for c in range(3)
        ],
        staged,
        outgoing,
    )
    exchange(outgoing, incoming, sems.at[0], sems.at[1], sems.at[2])
    rows = jnp.concatenate(unpack(incoming, staged), axis=1)
    both = dot(outer_high[...], rows) + dot(outer_low[...], rows)
    lane = lax.broadcasted_iota(jnp.int32, (PEERS, 128), 1)
    sign = jnp.where(lane < CELLS, 1.0, -1.0).astype(F32)
    spun = []
    for c in range(3):
        at = 128 * c
        upper, lower = both[:PEERS, at : at + 128], both[PEERS:, at : at + 128]
        if c == 0:
            upper, lower = upper + both[:PEERS, 384:], lower + both[PEERS:, 384:]
        value = upper + swapped(lower) * sign
        spun.append(value * twiddle[0] + swapped(value) * twiddle[1])
    high, low = split(jnp.concatenate(spun, axis=0))
    modes = dot(high, inner_high[...]) + (dot(low, inner_high[...]) + dot(high, inner_low[...]))
    slot = gy * GZ + gz
    wave_x = slot.astype(F32)
    wave_y, wave_z = waves[0], waves[1]
    squared = wave_x * wave_x + wave_y * wave_y + wave_z * wave_z
    inverse = jnp.where(squared > 0, 1.0 / jnp.maximum(squared, 1.0), 0.0)
    parts = [modes[PEERS * c : PEERS * (c + 1)] for c in range(3)]
    potential = (wave_x * parts[0] + wave_y * parts[1] + wave_z * parts[2]) * inverse
    weight = jnp.where(slot == 0, 1.0, 2.0).astype(F32) / (NL * 128.0 * 128.0)
    parts = [
        (part - wave * potential) * weight for part, wave in zip(parts, (wave_x, wave_y, wave_z))
    ]
    high, low = split(jnp.concatenate(parts, axis=0))
    near = dot(high, back_high[...]) + (dot(low, back_high[...]) + dot(high, back_low[...]))
    spun = []
    for c in range(3):
        value = near[PEERS * c : PEERS * (c + 1)]
        spun.append(value * twiddle[0] - swapped(value) * twiddle[1])
    high, low = split(jnp.concatenate(spun, axis=1))
    both = dot(outer_high[...], high) + (dot(outer_high[...], low) + dot(outer_low[...], high))
    pack(
        [
            both[:PEERS, 128 * c : 128 * (c + 1)] - swapped(both[PEERS:, 128 * c : 128 * (c + 1)]) * sign
            for c in range(3)
        ],
        staged,
        outgoing_back,
    )
    exchange(outgoing_back, incoming_back, sems.at[3], sems.at[4], sems.at[5])
    rows = [value.astype(F32) for value in unpack(incoming_back, staged)]
    real = jnp.concatenate([value[:, :CELLS] for value in rows], axis=1)
    imag = jnp.concatenate([value[:, CELLS:] for value in rows], axis=1)
    packed = jnp.concatenate([real, imag], axis=0).T.astype(BF)
    field = dot(packed, lines_high[...]) + dot(packed, lines_low[...])
    result[...] = jnp.concatenate(
        [field[:CELLS] + field[3 * CELLS :], field[CELLS : 3 * CELLS]], axis=0
    ).reshape(3, CELLS, NL)


def project(stepped, row_devices, depth_devices):
    tables = spectral_tables()
    vmem = pl.BlockSpec(memory_space=pltpu.VMEM)
    return pl.pallas_call(
        spectral,
        out_shape=jax.ShapeDtypeStruct(stepped.shape, F32),
        in_specs=[vmem] * (1 + len(tables)),
        out_specs=vmem,
        scratch_shapes=[
            pltpu.VMEM((4 * PEERS, 128), F32),
            *[pltpu.VMEM((PEERS, 4, 128), BF)] * 4,
            pltpu.SemaphoreType.DMA((6,)),
            pltpu.SemaphoreType.REGULAR,
        ],
        compiler_params=pltpu.CompilerParams(
            collective_id=0, has_side_effects=True, vmem_limit_bytes=48 * 2**20
        ),
    )(stepped, *tables)


def periodic_convolution(source, weight):
    channels = source.shape[0]
    inner_rows = source.shape[1] - 2
    inner_depth = source.shape[2] - 2
    stacked = jnp.concatenate([jnp.roll(source, 1 - offset, axis=3) for offset in range(3)], axis=0)
    matrices = jnp.transpose(weight, (0, 2, 3, 4, 1)).reshape(weight.shape[0], 3, 3, 3 * channels)
    partial_sums = []
    for first_shift in range(3):
        for second_shift in range(3):
            window = stacked[
                :,
                first_shift : first_shift + inner_rows,
                second_shift : second_shift + inner_depth,
                :,
            ]
            partial_sums.append(
                jnp.einsum(
                    "ok,kyzx->oyzx",
                    matrices[:, first_shift, second_shift],
                    window,
                    preferred_element_type=jnp.float32,
                )
            )
    return reduce(jnp.add, partial_sums)


def tendency(extended, learned_first, learned_rest, spacings):
    center = extended[:, 1:-1, 1:-1]
    flux_first = center * center[0:1] + learned_first
    divergence = (jnp.roll(flux_first, -1, axis=3) - jnp.roll(flux_first, 1, axis=3)) / (
        2.0 * spacings[0]
    )
    column = extended[:, :, 1:-1]
    flux_second = column * column[1:2] + learned_rest[:, 0, :, 1:-1]
    divergence = divergence + (flux_second[:, 2:] - flux_second[:, :-2]) / (2.0 * spacings[1])
    planes = extended[:, 1:-1, :]
    flux_third = planes * planes[2:3] + learned_rest[:, 1, 1:-1, :]
    divergence = divergence + (flux_third[:, :, 2:] - flux_third[:, :, :-2]) / (2.0 * spacings[2])
    laplacian = (
        jnp.roll(center, -1, axis=3) + jnp.roll(center, 1, axis=3) - 2.0 * center
    ) / spacings[0] ** 2
    laplacian = (
        laplacian
        + (extended[:, 2:, 1:-1] + extended[:, :-2, 1:-1] - 2.0 * center) / spacings[1] ** 2
    )
    laplacian = (
        laplacian
        + (extended[:, 1:-1, 2:] + extended[:, 1:-1, :-2] - 2.0 * center) / spacings[2] ** 2
    )
    return viscosity * laplacian - divergence


def body(velocity, forcing, first_kernel, first_bias, second_kernel):
    row_devices = lax.axis_size("gy")
    depth_devices = lax.axis_size("gz")
    local_rows = velocity.shape[1]
    local_depth = velocity.shape[2]
    line_cells = velocity.shape[3]
    all_rows = local_rows * row_devices
    all_depth = local_depth * depth_devices
    spacings = (2.0 * math.pi / line_cells, 2.0 * math.pi / all_rows, 2.0 * math.pi / all_depth)
    bias_column = first_bias[:, None, None, None]
    extended = extended_2(velocity, (("gy", 1), ("gz", 2)), 1)
    hidden = jax.nn.silu(
        periodic_convolution(extended.astype(jnp.bfloat16), first_kernel) + bias_column
    ).astype(jnp.bfloat16)
    hidden_wide = extended_2(hidden, (("gy", 1), ("gz", 2)), 1)
    correction = periodic_convolution(hidden_wide, second_kernel).astype(jnp.bfloat16)
    correction = correction.reshape(3, 3, local_rows, local_depth, line_cells)
    learned_first = correction[:, 0]
    learned_rest = extended_2(correction[:, 1:], (("gy", 2), ("gz", 3)), 1)
    stepped = (
        velocity + time_step * tendency(extended, learned_first, learned_rest, spacings) + forcing
    )
    projected = project(stepped.reshape(3, local_rows * local_depth, line_cells), row_devices, depth_devices)
    return projected.reshape(stepped.shape)


def solution(mesh):
    placed = (P(None, "gy", "gz", None), P(None, "gy", "gz", None), P(), P(), P())
    return jax.shard_map(
        body, mesh=mesh, in_specs=placed, out_specs=P(None, "gy", "gz", None), check_vma=False
    )
```

time: 240 us -> 115 us (0.48); the launches traced: 235 us -> 115 us
  matrix products: 66.6 us -> 13.2 us
  Pallas kernels: 0 us -> 43.9 us
  blocking collectives: 42.6 us -> 0 us
  starting transfers between devices: 67.5 us -> 33.9 us
  waiting for transfers between devices: 36.1 us -> 9 us
  local copies, waits for them, and re-layouts: 12.7 us -> 9.42 us
  other arithmetic: 8.42 us -> 5.25 us
    dot_general x20 -> x0, matrix products: 53.4 us -> none  [contract(): return jnp.einsum(pattern, values, matrix, precision=highest)]
    pallas_call x0 -> x1, Pallas kernels: none -> 43.9 us  [project(): pl.pallas_call(spectral, out_shape=jax.ShapeDtypeStruct(stepped.shape, F3...]
    all_to_all x2 -> x0, blocking collectives: 42.6 us -> none  [the longest x1 24.8 us: body(): lax.all_to_all(leaving_lines, 'gy', split_axis=2, concat_axis=2, tiled=True)]
    all_to_all x2 -> x0, waiting for transfers between devices: 27.1 us -> none  [the longest x1 14.6 us: body(): lax.all_to_all(spectrum, 'gy', split_axis=3, concat_axis=2, tiled=True)]
    all_to_all x2 -> x0, starting transfers between devices: 24.6 us -> none  [the longest x1 17.4 us: body(): lax.all_to_all(row_spectrum, 'gz', split_axis=2, concat_axis=2, tiled=True)]
    ppermute x6, starting transfers between devices: 15.4 us -> 6.37 us  [extended_2(): lax.ppermute(lax.slice_in_dim(block, block.shape[dim] - width, None, axis...]
    another operation x9 -> x0, local copies, waits for them, and re-layouts: 3.88 us -> none  [the longest x1 0.98 us: body(): row_spectrum = jnp.stack([new_real, new_imag])]
  transfers between devices with their start and end apart: 14 -> 12, of which waited for: 11 -> 9; matrix products, arithmetic and copies ran while one was open for 2% -> 4% of each run, Pallas kernels for 0% -> 0%
where the time goes in v1:
time: 115 us
  Pallas kernels  43.9 us (38%)
  starting transfers between devices  33.9 us (29%)
  matrix products  13.2 us (11%)
  local copies, waits for them, and re-layouts  9.42 us (8%)
  waiting for transfers between devices  9 us (8%)
  other arithmetic  5.25 us (5%)
    pallas_call x1, Pallas kernels, project(): pl.pallas_call(spectral, out_shape=jax.ShapeDtypeStruct(stepped.shape, F3...  43.9 us
    ppermute x6, starting transfers between devices, extended_2(): lax.ppermute(lax.slice_in_dim(block, 0, width, axis=dim), axis, backward)  27.6 us
    dot_general x18, matrix products, periodic_convolution(): jnp.einsum('ok,kyzx->oyzx', matrices[:, first_shift, second_shift], windo...  13.2 us
    ppermute x6, waiting for transfers between devices, extended_2(): lax.ppermute(lax.slice_in_dim(block, block.shape[dim] - width, None, axis...  6.62 us
    ppermute x6, starting transfers between devices, extended_2(): lax.ppermute(lax.slice_in_dim(block, block.shape[dim] - width, None, axis...  6.37 us
    concatenate x2, other arithmetic, periodic_convolution(): jnp.concatenate([jnp.roll(source, 1 - offset, axis=3) for offset in range...  3.48 us
    unnamed x46, local copies, waits for them, and re-layouts  2.6 us
    ppermute x6, waiting for transfers between devices, extended_2(): lax.ppermute(lax.slice_in_dim(block, 0, width, axis=dim), axis, backward)  2.37 us
  transfers between devices with their start and end apart: 12, of which 9 were waited for; matrix products, arithmetic and copies ran while one was open for 4% of the time, Pallas kernels for 0%

profile of v1, /device:TPU:1, one launch (start us, length us, event | category | flops | bytes accessed | tf_op | source)
XLA Modules:
  0.0 115.2 jit_solution(3423877965542296373)
XLA Ops:
  0.0 0.9 fusion.75
  0.9 2.2 %collective-permute-start.1 = (f32[3,1,8,512]{3,2,1,0:T(8,128)S(1)}, f32[3,1,8,512]{3,2,1,0:T(8,128)S(1)}, u32[]{:S(2)}, u32[]{:S(2)}) collective-permute-start(f32[3,1,8,512]{3,2,1,0:T(8,128)S(1)} %get-tuple-element.41), channel_id=1, source_target_pairs={{0,16},{16,32},{32,48},{48,64},{64,80},{80,96},{96,112},{112,128},... | collective-permute-start | bytes 147464 | tf_op jit(solution)/shard_map/ppermute | solution.py:23
  3.1 5.4 %collective-permute-start = (f32[3,1,8,512]{3,2,1,0:T(8,128)S(1)}, f32[3,1,8,512]{3,2,1,0:T(8,128)S(1)}, u32[]{:S(2)}, u32[]{:S(2)}) collective-permute-start(f32[3,1,8,512]{3,2,1,0:T(8,128)S(1)} %get-tuple-element.40), channel_id=1, source_target_pairs={{16,0},{32,16},{48,32},{64,48},{80,64},{96,80},{112,96},{128,112},... | collective-permute-start | bytes 147464 | tf_op jit(solution)/shard_map/ppermute | solution.py:26
  8.5 0.9 slice_bitcast_fusion.4
  9.4 1.4 %fusion.74 = (f32[3,8,8,511]{3,2,1,0:T(8,128)S(1)}, f32[3,8,8,511]{3,2,1,0:T(8,128)S(1)}) fusion(f32[3,8,8,512]{3,2,1,0:T(8,128)} %param.15), kind=kLoop, calls=%fused_computation.118 | loop fusion | bytes 1569792 | tf_op jit(solution)/shard_map/jit(_roll_static)/slice | solution.py:304
  12.1 1.0 collective-permute-start.2
  13.1 1.2 %collective-permute-start.3 = (f32[3,10,1,512]{3,2,1,0:T(1,128)S(1)}, f32[3,10,1,512]{3,2,1,0:T(1,128)S(1)}, u32[]{:S(2)}, u32[]{:S(2)}) collective-permute-start(f32[3,10,1,512]{3,2,1,0:T(1,128)S(1)} %get-tuple-element.30), channel_id=1, source_target_pairs={{0,1},{1,2},{2,3},{3,4},{4,5},{5,6},{6,7},{7,8},{8,9},{9,10},{10,1... | collective-permute-start | bytes 184328 | tf_op jit(solution)/shard_map/ppermute | solution.py:23
  14.3 1.8 %collective-permute-done.2 = f32[3,10,1,512]{3,2,1,0:T(1,128)S(1)} collective-permute-done((f32[3,10,1,512]{3,2,1,0:T(1,128)S(1)}, f32[3,10,1,512]{3,2,1,0:T(1,128)S(1)}, u32[]{:S(2)}, u32[]{:S(2)}) %collective-permute-start.2) | collective-permute-done | bytes 61472 | tf_op jit(solution)/shard_map/ppermute | solution.py:26
  16.1 2.0 %collective-permute-done.3 = f32[3,10,1,512]{3,2,1,0:T(1,128)S(1)} collective-permute-done((f32[3,10,1,512]{3,2,1,0:T(1,128)S(1)}, f32[3,10,1,512]{3,2,1,0:T(1,128)S(1)}, u32[]{:S(2)}, u32[]{:S(2)}) %collective-permute-start.3) | collective-permute-done | bytes 61472 | tf_op jit(solution)/shard_map/ppermute | solution.py:23
  19.1 0.9 fusion.64
  24.2 2.5 %fusion.3 = bf16[16,8,8,512]{3,0,2,1:T(8,128)(2,1)S(1)} fusion(f32[8,8,512,16]{2,3,1,0:T(8,128)S(1)} %fusion.6, f32[8,8,512,16]{2,3,1,0:T(8,128)S(1)} %fusion.8, f32[8,8,512,16]{2,3,1,0:T(8,128)S(1)} %fusion.10, f32[8,8,512,16]{2,3,1,0:T(8,128)S(1)} %fusion.12, f32[8,8,512,16]{2,3,1,0:T(8,128)S(1)} %fusion.14, f32[8,8,512,16]{2,3,1,0:T(8,128)S(1)} %fusion.16, ...), kind=kOutput, calls=%fused_computation.7 | convolution fusion | flops 16777216 | bytes 18415968 | tf_op jit(solution)/shard_map/ok,kyzx->oyzx/dot_general | solution.py:281
  27.1 3.6 %collective-permute-start.5 = (bf16[16,1,8,512]{3,0,2,1:T(8,128)(2,1)S(1)}, bf16[16,1,8,512]{3,0,2,1:T(8,128)(2,1)S(1)}, u32[]{:S(2)}, u32[]{:S(2)}) collective-permute-start(bf16[16,1,8,512]{3,0,2,1:T(8,128)(2,1)S(1)} %get-tuple-element.21), channel_id=1, source_target_pairs={{16,0},{32,16},{48,32},{64,48},{80,64},{96,80},{112,96},{128,112},... | collective-permute-start | bytes 393224 | tf_op jit(solution)/shard_map/ppermute | solution.py:26
  30.8 2.2 %collective-permute-done.4 = bf16[16,1,8,512]{3,0,2,1:T(8,128)(2,1)S(1)} collective-permute-done((bf16[16,1,8,512]{3,0,2,1:T(8,128)(2,1)S(1)}, bf16[16,1,8,512]{3,0,2,1:T(8,128)(2,1)S(1)}, u32[]{:S(2)}, u32[]{:S(2)}) %collective-permute-start.4) | collective-permute-done | bytes 131104 | tf_op jit(solution)/shard_map/ppermute | solution.py:23
  33.0 2.4 %collective-permute-start.6 = (bf16[16,10,1,512]{3,0,2,1:T(8,128)(2,1)S(1)}, bf16[16,10,1,512]{3,0,2,1:T(8,128)(2,1)S(1)}, u32[]{:S(2)}, u32[]{:S(2)}) collective-permute-start(bf16[16,10,1,512]{3,0,2,1:T(8,128)(2,1)S(1)} %get-tuple-element.18), channel_id=1, source_target_pairs={{0,1},{1,2},{2,3},{3,4},{4,5},{5,6},{6,7},{7,8},{8,9},{9,10},{10,1... | collective-permute-start | bytes 491528 | tf_op jit(solution)/shard_map/ppermute | solution.py:23
  35.4 5.5 %collective-permute-start.7 = (bf16[16,10,1,512]{3,0,2,1:T(8,128)(2,1)S(1)}, bf16[16,10,1,512]{3,0,2,1:T(8,128)(2,1)S(1)}, u32[]{:S(2)}, u32[]{:S(2)}) collective-permute-start(bf16[16,10,1,512]{3,0,2,1:T(8,128)(2,1)S(1)} %get-tuple-element.19), channel_id=1, source_target_pairs={{1,0},{2,1},{3,2},{4,3},{5,4},{6,5},{7,6},{8,7},{9,8},{10,9},{11,1... | collective-permute-start | bytes 491528 | tf_op jit(solution)/shard_map/ppermute | solution.py:26
  40.9 0.8 collective-permute-done.6
  42.2 1.0 fusion.63
  43.4 3.1 %maximum_maximum_fusion = bf16[48,10,10,512]{3,0,2,1:T(8,128)(2,1)S(1)} fusion(bf16[16,10,10,1]{3,0,2,1:T(8,128)(2,1)S(1)} %get-tuple-element.6, bf16[16,10,10,511]{3,0,2,1:T(8,128)(2,1)S(1)} %get-tuple-element.8, bf16[16,10,1,512]{3,0,2,1:T(8,128)(2,1)S(1)} %collective-permute-done.7, bf16[16,1,8,512]{3,0,2,1:T(8,128)(2,1)S(1)} %collective-permute-done.5, ...), kind=kLoop, calls=%fused_computation | loop fusion | flops 44236800 | bytes 9830400 | tf_op jit(solution)/shard_map/concatenate | solution.py:269
  47.1 0.6 fusion.45
  47.6 0.6 fusion.46
  48.2 0.6 fusion.47
  48.8 0.6 fusion.48
  49.4 0.6 fusion.49
  50.5 0.6 fusion.51
  51.1 2.1 %fusion.4 = bf16[9,8,8,512]{3,0,2,1:T(8,128)(2,1)S(1)} fusion(bf16[48,10,10,512]{3,0,2,1:T(8,128)(2,1)S(1)} %maximum_maximum_fusion, f32[8,8,512,9]{2,3,1,0:T(8,128)S(1)} %fusion.44, f32[8,8,512,9]{2,3,1,0:T(8,128)S(1)} %fusion.45, f32[8,8,512,9]{2,3,1,0:T(8,128)S(1)} %fusion.46, f32[8,8,512,9]{2,3,1,0:T(8,128)S(1)} %fusion.47, ...), kind=kOutput, calls=%fused_computation.10 | convolution fusion | flops 30965760 | bytes 14943072 | tf_op jit(solution)/shard_map/ok,kyzx->oyzx/dot_general | solution.py:281
  54.2 3.9 %collective-permute-start.9 = (bf16[3,2,1,8,512]{4,3,2,0,1:T(8,128)(2,1)S(1)}, bf16[3,2,1,8,512]{4,3,2,0,1:T(8,128)(2,1)S(1)}, u32[]{:S(2)}, u32[]{:S(2)}) collective-permute-start(bf16[3,2,1,8,512]{4,3,2,0,1:T(8,128)(2,1)S(1)} %copy.147), channel_id=1, source_target_pairs={{16,0},{32,16},{48,32},{64,48},{80,64},{96,80},{112,96},{128,112},... | collective-permute-start | bytes 147464 | tf_op jit(solution)/shard_map/ppermute | solution.py:26
  58.2 1.0 collective-permute-done.8
  59.6 8.2 %collective-permute-start.11 = (bf16[3,2,10,1,512]{4,3,2,0,1:T(2,128)(2,1)S(1)}, bf16[3,2,10,1,512]{4,3,2,0,1:T(2,128)(2,1)S(1)}, u32[]{:S(2)}, u32[]{:S(2)}) collective-permute-start(bf16[3,2,10,1,512]{4,3,2,0,1:T(2,128)(2,1)S(1)} %get-tuple-element.25), channel_id=1, source_target_pairs={{1,0},{2,1},{3,2},{4,3},{5,4},{6,5},{7,6},{8,7},{9,8},{10,9},{11,1... | collective-permute-start | bytes 184328 | tf_op jit(solution)/shard_map/ppermute | solution.py:26
  67.9 0.7 collective-permute-done.10
  69.1 0.7 fusion.29.stepped
  70.5 43.9 %shard_map.145 = f32[3,64,512]{2,1,0:T(8,128)S(1)} custom-call(f32[3,64,512]{2,1,0:T(8,128)S(1)} %fusion.29.stepped, bf16[512,512]{1,0:T(8,128)(2,1)S(1)} %copy-done, bf16[512,512]{1,0:T(8,128)(2,1)S(1)} %copy-done.1, bf16[512,256]{1,0:T(8,128)(2,1)S(1)} %copy-done.2, bf16[512,256]{1,0:T(8,128)(2,1)S(1)} %copy-done.3, bf16[128,128]{1,0:T(8,128)(2,1)S(1)} %copy-done.6, ...), custom_call_target="tpu_custom_call" | custom-call | tf_op jit(solution)/shard_map/pallas_call | solution.py:248
  114.5 0.7 copy.190
  (91 shorter events, 11.5 us)
Async XLA Ops:
  0.0 10.8 %copy-start.10 = (f32[3,8,8,512]{3,2,1,0:T(8,128)S(1)}, f32[3,8,8,512]{3,2,1,0:T(8,128)}, u32[]{:S(2)}) copy-start(f32[3,8,8,512]{3,2,1,0:T(8,128)} %param.15) | copy-start | bytes 1179652
  0.0 10.9 %copy-start.13 = (bf16[16,3,3,3,3]{0,4,3,2,1:T(4,128)(2,1)S(1)}, bf16[16,3,3,3,3]{0,4,3,2,1:T(4,128)(2,1)}, u32[]{:S(2)}) copy-start(bf16[16,3,3,3,3]{0,4,3,2,1:T(4,128)(2,1)} %param.17) | copy-start | bytes 7780
  0.0 10.9 %copy-start.12 = (bf16[9,16,3,3,3]{1,4,3,2,0:T(4,128)(2,1)S(1)}, bf16[9,16,3,3,3]{1,4,3,2,0:T(4,128)(2,1)}, u32[]{:S(2)}) copy-start(bf16[9,16,3,3,3]{1,4,3,2,0:T(4,128)(2,1)} %param.19) | copy-start | bytes 23332
  0.9 11.0 %collective-permute-start.1 = (f32[3,1,8,512]{3,2,1,0:T(8,128)S(1)}, f32[3,1,8,512]{3,2,1,0:T(8,128)S(1)}, u32[]{:S(2)}, u32[]{:S(2)}) collective-permute-start(f32[3,1,8,512]{3,2,1,0:T(8,128)S(1)} %get-tuple-element.41), channel_id=1, source_target_pairs={{0,16},{16,32},{32,48},{48,64},{64,80},{80,96},{96,112},{112,128},... | collective-permute-start | bytes 147464 | tf_op jit(solution)/shard_map/ppermute | solution.py:23
  3.1 8.9 %collective-permute-start = (f32[3,1,8,512]{3,2,1,0:T(8,128)S(1)}, f32[3,1,8,512]{3,2,1,0:T(8,128)S(1)}, u32[]{:S(2)}, u32[]{:S(2)}) collective-permute-start(f32[3,1,8,512]{3,2,1,0:T(8,128)S(1)} %get-tuple-element.40), channel_id=1, source_target_pairs={{16,0},{32,16},{48,32},{64,48},{80,64},{96,80},{112,96},{128,112},... | collective-permute-start | bytes 147464 | tf_op jit(solution)/shard_map/ppermute | solution.py:26
  12.1 4.0 %collective-permute-start.2 = (f32[3,10,1,512]{3,2,1,0:T(1,128)S(1)}, f32[3,10,1,512]{3,2,1,0:T(1,128)S(1)}, u32[]{:S(2)}, u32[]{:S(2)}) collective-permute-start(f32[3,10,1,512]{3,2,1,0:T(1,128)S(1)} %get-tuple-element.31), channel_id=1, source_target_pairs={{1,0},{2,1},{3,2},{4,3},{5,4},{6,5},{7,6},{8,7},{9,8},{10,9},{11,1... | collective-permute-start | bytes 184328 | tf_op jit(solution)/shard_map/ppermute | solution.py:26
  13.1 5.0 %collective-permute-start.3 = (f32[3,10,1,512]{3,2,1,0:T(1,128)S(1)}, f32[3,10,1,512]{3,2,1,0:T(1,128)S(1)}, u32[]{:S(2)}, u32[]{:S(2)}) collective-permute-start(f32[3,10,1,512]{3,2,1,0:T(1,128)S(1)} %get-tuple-element.30), channel_id=1, source_target_pairs={{0,1},{1,2},{2,3},{3,4},{4,5},{5,6},{6,7},{7,8},{8,9},{9,10},{10,1... | collective-permute-start | bytes 184328 | tf_op jit(solution)/shard_map/ppermute | solution.py:23
  23.6 0.7 copy-start.14
  26.8 6.2 %collective-permute-start.4 = (bf16[16,1,8,512]{3,0,2,1:T(8,128)(2,1)S(1)}, bf16[16,1,8,512]{3,0,2,1:T(8,128)(2,1)S(1)}, u32[]{:S(2)}, u32[]{:S(2)}) collective-permute-start(bf16[16,1,8,512]{3,0,2,1:T(8,128)(2,1)S(1)} %get-tuple-element.20), channel_id=1, source_target_pairs={{0,16},{16,32},{32,48},{48,64},{64,80},{80,96},{96,112},{112,128},... | collective-permute-start | bytes 393224 | tf_op jit(solution)/shard_map/ppermute | solution.py:23
  27.1 5.9 %collective-permute-start.5 = (bf16[16,1,8,512]{3,0,2,1:T(8,128)(2,1)S(1)}, bf16[16,1,8,512]{3,0,2,1:T(8,128)(2,1)S(1)}, u32[]{:S(2)}, u32[]{:S(2)}) collective-permute-start(bf16[16,1,8,512]{3,0,2,1:T(8,128)(2,1)S(1)} %get-tuple-element.21), channel_id=1, source_target_pairs={{16,0},{32,16},{48,32},{64,48},{80,64},{96,80},{112,96},{128,112},... | collective-permute-start | bytes 393224 | tf_op jit(solution)/shard_map/ppermute | solution.py:26
  33.0 8.6 %collective-permute-start.6 = (bf16[16,10,1,512]{3,0,2,1:T(8,128)(2,1)S(1)}, bf16[16,10,1,512]{3,0,2,1:T(8,128)(2,1)S(1)}, u32[]{:S(2)}, u32[]{:S(2)}) collective-permute-start(bf16[16,10,1,512]{3,0,2,1:T(8,128)(2,1)S(1)} %get-tuple-element.18), channel_id=1, source_target_pairs={{0,1},{1,2},{2,3},{3,4},{4,5},{5,6},{6,7},{7,8},{8,9},{9,10},{10,1... | collective-permute-start | bytes 491528 | tf_op jit(solution)/shard_map/ppermute | solution.py:23
  35.4 6.5 %collective-permute-start.7 = (bf16[16,10,1,512]{3,0,2,1:T(8,128)(2,1)S(1)}, bf16[16,10,1,512]{3,0,2,1:T(8,128)(2,1)S(1)}, u32[]{:S(2)}, u32[]{:S(2)}) collective-permute-start(bf16[16,10,1,512]{3,0,2,1:T(8,128)(2,1)S(1)} %get-tuple-element.19), channel_id=1, source_target_pairs={{1,0},{2,1},{3,2},{4,3},{5,4},{6,5},{7,6},{8,7},{9,8},{10,9},{11,1... | collective-permute-start | bytes 491528 | tf_op jit(solution)/shard_map/ppermute | solution.py:26
  53.6 5.6 %collective-permute-start.8 = (bf16[3,2,1,8,512]{4,3,2,0,1:T(8,128)(2,1)S(1)}, bf16[3,2,1,8,512]{4,3,2,0,1:T(8,128)(2,1)S(1)}, u32[]{:S(2)}, u32[]{:S(2)}) collective-permute-start(bf16[3,2,1,8,512]{4,3,2,0,1:T(8,128)(2,1)S(1)} %copy.145), channel_id=1, source_target_pairs={{0,16},{16,32},{32,48},{48,64},{64,80},{80,96},{96,112},{112,128},... | collective-permute-start | bytes 147464 | tf_op jit(solution)/shard_map/ppermute | solution.py:23
  54.2 5.1 %collective-permute-start.9 = (bf16[3,2,1,8,512]{4,3,2,0,1:T(8,128)(2,1)S(1)}, bf16[3,2,1,8,512]{4,3,2,0,1:T(8,128)(2,1)S(1)}, u32[]{:S(2)}, u32[]{:S(2)}) collective-permute-start(bf16[3,2,1,8,512]{4,3,2,0,1:T(8,128)(2,1)S(1)} %copy.147), channel_id=1, source_target_pairs={{16,0},{32,16},{48,32},{64,48},{80,64},{96,80},{112,96},{128,112},... | collective-permute-start | bytes 147464 | tf_op jit(solution)/shard_map/ppermute | solution.py:26
  59.5 9.5 %copy-start.11 = (f32[3,8,8,512]{3,2,1,0:T(8,128)S(1)}, f32[3,8,8,512]{3,2,1,0:T(8,128)}, u32[]{:S(2)}) copy-start(f32[3,8,8,512]{3,2,1,0:T(8,128)} %param.16) | copy-start | bytes 1179652
  59.5 9.0 %collective-permute-start.10 = (bf16[3,2,10,1,512]{4,3,2,0,1:T(2,128)(2,1)S(1)}, bf16[3,2,10,1,512]{4,3,2,0,1:T(2,128)(2,1)S(1)}, u32[]{:S(2)}, u32[]{:S(2)}) collective-permute-start(bf16[3,2,10,1,512]{4,3,2,0,1:T(2,128)(2,1)S(1)} %get-tuple-element.24), channel_id=1, source_target_pairs={{0,1},{1,2},{2,3},{3,4},{4,5},{5,6},{6,7},{7,8},{8,9},{9,10},{10,1... | collective-permute-start | bytes 184328 | tf_op jit(solution)/shard_map/ppermute | solution.py:23
  59.6 9.2 %collective-permute-start.11 = (bf16[3,2,10,1,512]{4,3,2,0,1:T(2,128)(2,1)S(1)}, bf16[3,2,10,1,512]{4,3,2,0,1:T(2,128)(2,1)S(1)}, u32[]{:S(2)}, u32[]{:S(2)}) collective-permute-start(bf16[3,2,10,1,512]{4,3,2,0,1:T(2,128)(2,1)S(1)} %get-tuple-element.25), channel_id=1, source_target_pairs={{1,0},{2,1},{3,2},{4,3},{5,4},{6,5},{7,6},{8,7},{9,8},{10,9},{11,1... | collective-permute-start | bytes 184328 | tf_op jit(solution)/shard_map/ppermute | solution.py:26
  69.0 1.0 copy-start
  69.0 1.2 %copy-start.1 = (bf16[512,512]{1,0:T(8,128)(2,1)S(1)}, bf16[512,512]{1,0:T(8,128)(2,1)}, u32[]{:S(2)}) copy-start(bf16[512,512]{1,0:T(8,128)(2,1)} %constant.44.clone.lines_low) | copy-start | bytes 1572868
  69.0 1.2 %copy-start.2 = (bf16[512,256]{1,0:T(8,128)(2,1)S(1)}, bf16[512,256]{1,0:T(8,128)(2,1)}, u32[]{:S(2)}) copy-start(bf16[512,256]{1,0:T(8,128)(2,1)} %constant.45.clone.outer_high) | copy-start | bytes 786436
  69.0 1.3 %copy-start.3 = (bf16[512,256]{1,0:T(8,128)(2,1)S(1)}, bf16[512,256]{1,0:T(8,128)(2,1)}, u32[]{:S(2)}) copy-start(bf16[512,256]{1,0:T(8,128)(2,1)} %constant.46.clone.outer_low) | copy-start | bytes 786436
  69.1 1.4 %copy-start.4 = (f32[2,256,128]{2,1,0:T(8,128)S(1)}, f32[2,256,128]{2,1,0:T(8,128)}, u32[]{:S(2)}) copy-start(f32[2,256,128]{2,1,0:T(8,128)} %constant.51.clone.twiddle) | copy-start | bytes 786436
  69.1 1.5 %copy-start.5 = (f32[2,256,128]{2,1,0:T(8,128)S(1)}, f32[2,256,128]{2,1,0:T(8,128)}, u32[]{:S(2)}) copy-start(f32[2,256,128]{2,1,0:T(8,128)} %constant.52.clone.waves) | copy-start | bytes 786436
  69.1 1.4 %copy-start.6 = (bf16[128,128]{1,0:T(8,128)(2,1)S(1)}, bf16[128,128]{1,0:T(8,128)(2,1)}, u32[]{:S(2)}) copy-start(bf16[128,128]{1,0:T(8,128)(2,1)} %constant.47.clone.inner_high) | copy-start | bytes 98308
  69.1 1.4 %copy-start.7 = (bf16[128,128]{1,0:T(8,128)(2,1)S(1)}, bf16[128,128]{1,0:T(8,128)(2,1)}, u32[]{:S(2)}) copy-start(bf16[128,128]{1,0:T(8,128)(2,1)} %constant.48.clone.inner_low) | copy-start | bytes 98308
  69.1 1.4 %copy-start.8 = (bf16[128,128]{1,0:T(8,128)(2,1)S(1)}, bf16[128,128]{1,0:T(8,128)(2,1)}, u32[]{:S(2)}) copy-start(bf16[128,128]{1,0:T(8,128)(2,1)} %constant.49.clone.back_high) | copy-start | bytes 98308
  69.1 1.4 %copy-start.9 = (bf16[128,128]{1,0:T(8,128)(2,1)S(1)}, bf16[128,128]{1,0:T(8,128)(2,1)}, u32[]{:S(2)}) copy-start(bf16[128,128]{1,0:T(8,128)(2,1)} %constant.50.clone.back_low) | copy-start | bytes 98308

commit v2 on v1

--- a/solution.py
+++ b/solution.py
@@ -1,4 +1,3 @@
-from functools import reduce
 import math
 
 import jax
@@ -11,23 +10,6 @@
 
 time_step = 0.02
 viscosity = 0.002
-highest = lax.Precision.HIGHEST
-
-
-def extended_2(block, sides, width):
-    for axis, dim in sides:
-        count = lax.axis_size(axis)
-        forward = [(i, i + 1) for i in range(count - 1)]
-        forward.append((count - 1, 0))
-        backward = [(target, source) for source, target in forward]
-        low = lax.ppermute(
-            lax.slice_in_dim(block, block.shape[dim] - width, None, axis=dim), axis, forward
-        )
-        high = lax.ppermute(lax.slice_in_dim(block, 0, width, axis=dim), axis, backward)
-        block = jnp.concatenate([low, block, high], axis=dim)
-    return block
-
-
 MESH = pl.DeviceIdType.MESH
 BF = jnp.bfloat16
 F32 = jnp.float32
@@ -91,7 +73,7 @@
     return lax.dot_general(left, right, (dims, ((), ())), preferred_element_type=F32)
 
 
-def enter(ready):
+def greet_all():
     gy, gz = lax.axis_index("gy"), lax.axis_index("gz")
     barrier = pltpu.get_barrier_semaphore()
 
@@ -101,7 +83,11 @@
         return carry
 
     lax.fori_loop(1, 16, greet, 0)
-    pl.semaphore_wait(barrier, GY + GZ - 2)
+
+
+def meet_all(ready):
+    gy, gz = lax.axis_index("gy"), lax.axis_index("gz")
+    pl.semaphore_wait(pltpu.get_barrier_semaphore(), GY + GZ - 2)
 
     def confirm(step, carry):
         pl.semaphore_signal(ready, inc=1, device_id=(gy, lax.rem(gz + step, GZ)), device_id_type=MESH)
@@ -152,8 +138,186 @@
     return pltpu.roll(value, CELLS, axis=1)
 
 
-def spectral(
-    stepped,
+WIDE = 14
+SPAN = 3 * 4 * WIDE
+HIDDEN = 16
+
+
+def neighbours():
+    return [(a, b) for a in (-1, 0, 1) for b in (-1, 0, 1) if (a, b) != (0, 0)]
+
+
+def span(side, sending):
+    if side == 0:
+        return pl.ds(0, 8) if sending else pl.ds(3, 8)
+    if side < 0:
+        return pl.ds(0, 3) if sending else pl.ds(WIDE - 3, 3)
+    return pl.ds(5, 3) if sending else pl.ds(0, 3)
+
+
+def halo(edge, around, sems):
+    gy, gz = lax.axis_index("gy"), lax.axis_index("gz")
+    copies = []
+    for index, (a, b) in enumerate(neighbours()):
+        copies.append(
+            pltpu.make_async_remote_copy(
+                edge.at[span(a, True), span(b, True)],
+                around.at[span(a, False), span(b, False)],
+                sems.at[index],
+                sems.at[8 + index],
+                device_id=(lax.rem(gy + a + GY, GY), lax.rem(gz + b + GZ, GZ)),
+                device_id_type=MESH,
+            )
+        )
+    for copy in copies:
+        copy.start()
+    return copies
+
+
+def taken(cells, y, rows):
+    return jnp.concatenate([cells[y, t, rows, :] for t in range(4)], axis=1)
+
+
+def put(cells, y, rows, value):
+    for t in range(4):
+        cells[y, t, rows, :] = value[:, 128 * t : 128 * (t + 1)]
+
+
+def prepare(velocity, first, second, cells, edge, first_matrix, second_rows, second_matrix):
+    def place(y, carry):
+        for c in range(4):
+            value = velocity[c, y] if c < 3 else jnp.zeros((8, NL), F32)
+            for t in range(4):
+                cells[y + 3, t, pl.ds(12 + c, 8, stride=4), :] = value[:, 128 * t : 128 * (t + 1)]
+        edge[y] = taken(cells, y + 3, pl.ds(12, 32)).astype(BF).reshape(8, 4, NL)
+        return carry
+
+    lax.fori_loop(0, 8, place, 0)
+    for z in range(12):
+        rows = first[...] if z == 0 else pltpu.roll(first[...], 4 * z, axis=1)
+        first_matrix[pl.ds(HIDDEN * z, HIDDEN), :] = rows.astype(BF)
+    for z in range(8):
+        rows = second[...] if z == 0 else pltpu.roll(second[...], HIDDEN * z, axis=1)
+        for t in range(5):
+            second_rows[t, pl.ds(z, 27, stride=8), :] = rows[:27, 128 * t : 128 * (t + 1)]
+    second_matrix[...] = jnp.concatenate([second_rows[t] for t in range(5)], axis=1)[:, : 36 * HIDDEN].astype(BF)
+
+
+def spread(around, cells, stacked):
+    for y in (*range(3), *range(WIDE - 3, WIDE)):
+        put(cells, y, pl.ds(0, 4 * WIDE), around[y].astype(F32).reshape(4 * WIDE, NL))
+
+    def sides(y, carry):
+        put(cells, y, pl.ds(0, 12), around[y, pl.ds(0, 3)].astype(F32).reshape(12, NL))
+        put(cells, y, pl.ds(44, 12), around[y, pl.ds(11, 3)].astype(F32).reshape(12, NL))
+        return carry
+
+    lax.fori_loop(3, 11, sides, 0)
+
+    def stack(y, carry):
+        row = taken(cells, y, pl.ds(0, 4 * WIDE))
+        at = y * SPAN
+        stacked[pl.ds(pl.multiple_of(at, 8), 56), :] = pltpu.roll(row, 1, axis=1)
+        stacked[pl.ds(pl.multiple_of(at + 56, 8), 56), :] = row
+        stacked[pl.ds(pl.multiple_of(at + 112, 8), 56), :] = pltpu.roll(row, NL - 1, axis=1)
+        return carry
+
+    lax.fori_loop(0, WIDE, stack, 0)
+    stacked[pl.ds(WIDE * SPAN, 8), :] = jnp.zeros((8, NL), F32)
+
+
+def correct(bias, stacked, first_matrix, second_matrix, learned):
+    learned[0] = jnp.zeros((72, NL), F32)
+    learned[1] = jnp.zeros((72, NL), F32)
+
+    def layer(y, carry):
+        source = stacked[pl.ds(pl.multiple_of(y * SPAN, 8), 512), :].astype(BF)
+        before = dot(first_matrix[...], source) + bias[...]
+        hidden = before * (0.5 + 0.5 * jnp.tanh(0.5 * before))
+        wide = jnp.concatenate(
+            [
+                pltpu.roll(hidden, 1, axis=1).astype(BF),
+                hidden.astype(BF),
+                pltpu.roll(hidden, NL - 1, axis=1).astype(BF),
+            ],
+            axis=0,
+        )
+        part = dot(second_matrix[...], wide)
+        learned[y + 2] = part[:72]
+        learned[y + 1] += part[72:144]
+        learned[y] += part[144:]
+        return carry
+
+    lax.fori_loop(0, 12, layer, 0)
+
+
+def advance(velocity, forcing, cells, learned, stepped):
+    steps = (2.0 * math.pi / NL, 2.0 * math.pi / 128, 2.0 * math.pi / 128)
+    half = [0.5 / h for h in steps]
+    square = [1.0 / h**2 for h in steps]
+
+    def ahead(value):
+        return pltpu.roll(value, NL - 1, axis=1)
+
+    def behind(value):
+        return pltpu.roll(value, 1, axis=1)
+
+    def lines(y, c, z):
+        return taken(cells, y, pl.ds(12 + 4 * z + c, 8, stride=4))
+
+    def move(y, carry):
+        here = [velocity[c, y] for c in range(3)]
+        over = [lines(y + 4, c, 0) for c in range(3)]
+        under = [lines(y + 2, c, 0) for c in range(3)]
+        far = [lines(y + 3, c, 1) for c in range(3)]
+        near = [lines(y + 3, c, -1) for c in range(3)]
+        for i in range(3):
+            first = here[i] * here[0] + learned[y + 3, pl.ds(8 * i, 8), :].astype(BF).astype(F32)
+            rows = pl.ds(24 + 8 * i, 8)
+            second = (over[i] * over[1] + learned[y + 4, rows, :]) - (
+                under[i] * under[1] + learned[y + 2, rows, :]
+            )
+            third = (far[i] * far[2] - near[i] * near[2]) + learned[y + 3, pl.ds(48 + 8 * i, 8), :]
+            divergence = (
+                (ahead(first) - behind(first)) * half[0] + second * half[1] + third * half[2]
+            )
+            twice = 2.0 * here[i]
+            laplacian = (
+                (ahead(here[i]) + behind(here[i]) - twice) * square[0]
+                + (over[i] + under[i] - twice) * square[1]
+                + (far[i] + near[i] - twice) * square[2]
+            )
+            stepped[i, pl.ds(pl.multiple_of(8 * y, 8), 8), :] = (
+                here[i] + time_step * (viscosity * laplacian - divergence) + forcing[i, y]
+            )
+        return carry
+
+    lax.fori_loop(0, 8, move, 0)
+
+
+def first_rows(kernel):
+    rows = jnp.transpose(kernel, (0, 2, 4, 3, 1)).astype(F32)
+    rows = jnp.pad(rows, ((0, 0), (0, 0), (0, 0), (0, WIDE - 3), (0, 1)))
+    return jnp.pad(rows.reshape(HIDDEN, 9 * 4 * WIDE), ((0, 0), (0, 8)))
+
+
+def second_rows_of(kernel):
+    taps = kernel.astype(F32).reshape(3, 3, HIDDEN, 3, 3, 3)
+    taps = jnp.transpose(taps, (3, 1, 0, 5, 4, 2))
+    quiet = ((0, 0),) * 4
+    middle = jnp.pad(taps[:, :2], (*quiet, (1, 1), (0, 0)))
+    slope = jnp.pad(taps[:, 2:], (*quiet, (2, 0), (0, 0))) - jnp.pad(taps[:, 2:], (*quiet, (0, 2), (0, 0)))
+    rows = jnp.concatenate([middle, slope], axis=1)
+    rows = jnp.pad(rows, (*quiet, (0, 7), (0, 0))).reshape(27, 36 * HIDDEN)
+    return jnp.pad(rows, ((0, 5), (0, 4 * HIDDEN)))
+
+
+def whole(
+    velocity,
+    forcing,
+    first,
+    bias,
+    second,
     lines_high,
     lines_low,
     outer_high,
@@ -165,15 +329,33 @@
     twiddle,
     waves,
     result,
+    cells,
+    edge,
+    around,
+    stacked,
+    first_matrix,
+    second_rows,
+    second_matrix,
+    learned,
+    stepped,
     staged,
     outgoing,
     incoming,
     outgoing_back,
     incoming_back,
+    halo_sems,
     sems,
     ready,
 ):
-    enter(ready)
+    greet_all()
+    prepare(velocity, first, second, cells, edge, first_matrix, second_rows, second_matrix)
+    meet_all(ready)
+    copies = halo(edge, around, halo_sems)
+    for copy in copies:
+        copy.wait()
+    spread(around, cells, stacked)
+    correct(bias, stacked, first_matrix, second_matrix, learned)
+    advance(velocity, forcing, cells, learned, stepped)
     gy, gz = lax.axis_index("gy"), lax.axis_index("gz")
     nt = ((1,), (1,))
     high, low = split(stepped[...].reshape(3 * CELLS, NL))
@@ -242,102 +424,36 @@
     ).reshape(3, CELLS, NL)
 
 
-def project(stepped, row_devices, depth_devices):
+def body(velocity, forcing, first_kernel, first_bias, second_kernel):
     tables = spectral_tables()
     vmem = pl.BlockSpec(memory_space=pltpu.VMEM)
-    return pl.pallas_call(
-        spectral,
-        out_shape=jax.ShapeDtypeStruct(stepped.shape, F32),
-        in_specs=[vmem] * (1 + len(tables)),
+    bias = jnp.broadcast_to(first_bias[None, :], (12, HIDDEN)).reshape(12 * HIDDEN, 1)
+    field = pl.pallas_call(
+        whole,
+        out_shape=jax.ShapeDtypeStruct((3, CELLS, NL), F32),
+        in_specs=[vmem] * (5 + len(tables)),
         out_specs=vmem,
         scratch_shapes=[
+            pltpu.VMEM((WIDE, 4, 4 * WIDE, 128), F32),
+            pltpu.VMEM((8, 8, 4, NL), BF),
+            pltpu.VMEM((WIDE, WIDE, 4, NL), BF),
+            pltpu.VMEM((WIDE * SPAN + 8, NL), F32),
+            pltpu.VMEM((12 * HIDDEN, 512), BF),
+            pltpu.VMEM((5, 216, 128), F32),
+            pltpu.VMEM((216, 36 * HIDDEN), BF),
+            pltpu.VMEM((WIDE, 72, NL), F32),
+            pltpu.VMEM((3, CELLS, NL), F32),
             pltpu.VMEM((4 * PEERS, 128), F32),
             *[pltpu.VMEM((PEERS, 4, 128), BF)] * 4,
+            pltpu.SemaphoreType.DMA((16,)),
             pltpu.SemaphoreType.DMA((6,)),
             pltpu.SemaphoreType.REGULAR,
         ],
         compiler_params=pltpu.CompilerParams(
-            collective_id=0, has_side_effects=True, vmem_limit_bytes=48 * 2**20
+            collective_id=0, has_side_effects=True, vmem_limit_bytes=56 * 2**20
         ),
-    )(stepped, *tables)
-
-
-def periodic_convolution(source, weight):
-    channels = source.shape[0]
-    inner_rows = source.shape[1] - 2
-    inner_depth = source.shape[2] - 2
-    stacked = jnp.concatenate([jnp.roll(source, 1 - offset, axis=3) for offset in range(3)], axis=0)
-    matrices = jnp.transpose(weight, (0, 2, 3, 4, 1)).reshape(weight.shape[0], 3, 3, 3 * channels)
-    partial_sums = []
-    for first_shift in range(3):
-        for second_shift in range(3):
-            window = stacked[
-                :,
-                first_shift : first_shift + inner_rows,
-                second_shift : second_shift + inner_depth,
-                :,
-            ]
-            partial_sums.append(
-                jnp.einsum(
-                    "ok,kyzx->oyzx",
-                    matrices[:, first_shift, second_shift],
-                    window,
-                    preferred_element_type=jnp.float32,
-                )
-            )
-    return reduce(jnp.add, partial_sums)
-
-
-def tendency(extended, learned_first, learned_rest, spacings):
-    center = extended[:, 1:-1, 1:-1]
-    flux_first = center * center[0:1] + learned_first
-    divergence = (jnp.roll(flux_first, -1, axis=3) - jnp.roll(flux_first, 1, axis=3)) / (
-        2.0 * spacings[0]
-    )
-    column = extended[:, :, 1:-1]
-    flux_second = column * column[1:2] + learned_rest[:, 0, :, 1:-1]
-    divergence = divergence + (flux_second[:, 2:] - flux_second[:, :-2]) / (2.0 * spacings[1])
-    planes = extended[:, 1:-1, :]
-    flux_third = planes * planes[2:3] + learned_rest[:, 1, 1:-1, :]
-    divergence = divergence + (flux_third[:, :, 2:] - flux_third[:, :, :-2]) / (2.0 * spacings[2])
-    laplacian = (
-        jnp.roll(center, -1, axis=3) + jnp.roll(center, 1, axis=3) - 2.0 * center
-    ) / spacings[0] ** 2
-    laplacian = (
-        laplacian
-        + (extended[:, 2:, 1:-1] + extended[:, :-2, 1:-1] - 2.0 * center) / spacings[1] ** 2
-    )
-    laplacian = (
-        laplacian
-        + (extended[:, 1:-1, 2:] + extended[:, 1:-1, :-2] - 2.0 * center) / spacings[2] ** 2
-    )
-    return viscosity * laplacian - divergence
-
-
-def body(velocity, forcing, first_kernel, first_bias, second_kernel):
-    row_devices = lax.axis_size("gy")
-    depth_devices = lax.axis_size("gz")
-    local_rows = velocity.shape[1]
-    local_depth = velocity.shape[2]
-    line_cells = velocity.shape[3]
-    all_rows = local_rows * row_devices
-    all_depth = local_depth * depth_devices
-    spacings = (2.0 * math.pi / line_cells, 2.0 * math.pi / all_rows, 2.0 * math.pi / all_depth)
-    bias_column = first_bias[:, None, None, None]
-    extended = extended_2(velocity, (("gy", 1), ("gz", 2)), 1)
-    hidden = jax.nn.silu(
-        periodic_convolution(extended.astype(jnp.bfloat16), first_kernel) + bias_column
-    ).astype(jnp.bfloat16)
-    hidden_wide = extended_2(hidden, (("gy", 1), ("gz", 2)), 1)
-    correction = periodic_convolution(hidden_wide, second_kernel).astype(jnp.bfloat16)
-    correction = correction.reshape(3, 3, local_rows, local_depth, line_cells)
-    learned_first = correction[:, 0]
-    learned_rest = extended_2(correction[:, 1:], (("gy", 2), ("gz", 3)), 1)
-    stepped = (
-        velocity + time_step * tendency(extended, learned_first, learned_rest, spacings) + forcing
-    )
-    projected = project(stepped.reshape(3, local_rows * local_depth, line_cells), row_devices, depth_devices)
-    return projected.reshape(stepped.shape)
+    )(velocity, forcing, first_rows(first_kernel), bias, second_rows_of(second_kernel), *tables)
+    return field.reshape(velocity.shape)
 
 
 def solution(mesh):

time: 115 us -> 69.3 us (0.60)
  starting transfers between devices: 33.9 us -> 0 us
  Pallas kernels: 43.9 us -> 63.6 us
  matrix products: 13.2 us -> 0 us
  waiting for transfers between devices: 9 us -> 0 us
  local copies, waits for them, and re-layouts: 9.42 us -> 4.7 us
  other arithmetic: 5.25 us -> 0.71 us
    ppermute x12 -> x0, starting transfers between devices: 33.9 us -> none  [the longest x6 27.6 us: extended_2(): lax.ppermute(lax.slice_in_dim(block, 0, width, axis=dim), axis, backward)]
    pallas_call x1, Pallas kernels: 43.9 us -> 63.6 us  [body(): pl.pallas_call(whole, out_shape=jax.ShapeDtypeStruct((3, CELLS, NL), F32)...]
    dot_general x18 -> x0, matrix products: 13.2 us -> none  [periodic_convolution(): jnp.einsum('ok,kyzx->oyzx', matrices[:, first_shift, second_shift], windo...]
    ppermute x12 -> x0, waiting for transfers between devices: 9 us -> none  [the longest x6 6.62 us: extended_2(): lax.ppermute(lax.slice_in_dim(block, block.shape[dim] - width, None, axis...]
    slice x16 -> x2, local copies, waits for them, and re-layouts: 5.37 us -> 0.03 us  [the longest x1 0.02 us: second_rows_of(): middle = jnp.pad(taps[:, :2], (*quiet, (1, 1), (0, 0)))]
    concatenate x4 -> x1, other arithmetic: 3.97 us -> 0.05 us  [second_rows_of(): rows = jnp.concatenate([middle, slope], axis=1)]
    unnamed x46 -> x6, local copies, waits for them, and re-layouts: 2.6 us -> 1.92 us
  transfers between devices with their start and end apart: 12 -> 0, of which waited for: 9 -> 0; matrix products, arithmetic and copies ran while one was open for 4% -> 0% of each run, Pallas kernels for 0% -> 0%
where the time goes in v2:
time: 69.3 us; the launch traced here: 69.1 us
  Pallas kernels  63.6 us (92%)
  local copies, waits for them, and re-layouts  4.7 us (7%)
  other arithmetic  0.71 us (1%)
    pallas_call x1, Pallas kernels, body(): pl.pallas_call(whole, out_shape=jax.ShapeDtypeStruct((3, CELLS, NL), F32)...  63.6 us
    unnamed x6, local copies, waits for them, and re-layouts  1.92 us

profile of v2, /device:TPU:1, one launch (start us, length us, event | category | flops | bytes accessed | tf_op | source)
XLA Modules:
  0.0 69.1 jit_solution(10551772579422888559)
XLA Ops:
  0.0 0.9 %copy.24 = f32[3,3,16,3,3,3]{2,4,5,0,1,3:T(4,128)S(1)} copy(bf16[3,3,16,3,3,3]{2,5,4,3,1,0:T(4,128)(2,1)} %bitcast.12) | data formatting | bytes 23328 | tf_op jit(solution)/shard_map/transpose | solution.py:306
  1.0 0.1 select_maximum_fusion
  1.1 0.2 reshape.21
  1.4 0.0 copy-start
  1.4 0.6 pad.38.second
  2.0 0.1 copy-done
  2.2 0.1 copy.19
  2.3 0.0 copy-start.1
  2.3 0.6 pad_convert_fusion.first
  2.9 0.0 copy-done.1
  3.0 0.7 %reshape.24.bias = f32[192,1]{1,0:T(8,128)} reshape(f32[12,16]{1,0:T(8,128)S(1)} %broadcast_in_dim.2) | data formatting | bytes 1536 | tf_op jit(solution)/shard_map/reshape | solution.py:430
  3.7 63.6 %shard_map.145 = f32[3,64,512]{2,1,0:T(8,128)} custom-call(f32[3,8,8,512]{3,2,1,0:T(8,128)} %velocity.1, f32[3,8,8,512]{3,2,1,0:T(8,128)} %forcing.1, f32[16,512]{1,0:T(8,128)} %pad_convert_fusion.first, f32[192,1]{1,0:T(8,128)} %reshape.24.bias, f32[32,640]{1,0:T(8,128)} %pad.38.second, bf16[512,512]{1,0:T(8,128)(2,1)} %constant.25.clone.lines_high, ...), custom_call_target="tpu_custom_call" | custom-call | tf_op jit(solution)/shard_map/pallas_call | solution.py:431
  67.3 1.8 %copy.26 = f32[3,8,8,512]{3,2,1,0:T(8,128)} copy(f32[3,8,8,512]{3,2,1,0:T(8,128)} %bitcast.8) | data formatting | bytes 786432
  (7 shorter events, 0.2 us)
Async XLA Ops:
  1.4 0.7 %copy-start = (bf16[16,3,3,3,3]{0,4,3,2,1:T(4,128)(2,1)S(1)}, bf16[16,3,3,3,3]{0,4,3,2,1:T(4,128)(2,1)}, u32[]{:S(2)}) copy-start(bf16[16,3,3,3,3]{0,4,3,2,1:T(4,128)(2,1)} %param.17) | copy-start | bytes 7780
  2.3 0.7 copy-start.1

commit v3 on v2

--- a/solution.py
+++ b/solution.py
@@ -10,6 +10,10 @@
 
 time_step = 0.02
 viscosity = 0.002
+UNROLL_PLACE = 2
+UNROLL_STACK = 2
+UNROLL_LAYER = 2
+FAR = (4, 3, 5, 2, 6, 1, 7, 0)
 MESH = pl.DeviceIdType.MESH
 BF = jnp.bfloat16
 F32 = jnp.float32
@@ -54,14 +58,18 @@
     sign = np.where(lane < CELLS, 1.0, -1.0)[None, :]
     twiddle = np.stack([np.cos(turn), np.sin(turn) * sign]).astype(np.float32)
 
+    return (*halves(lines), *halves(outer), *halves(inner), *halves(inner.T.copy()), twiddle)
+
+
+def signed_waves():
+    row = lax.broadcasted_iota(jnp.int32, (PEERS, 128), 0)
+    lane = lax.rem(lax.broadcasted_iota(jnp.int32, (PEERS, 128), 1), CELLS)
+
     def signed(index):
-        wave = np.where(2 * index > 128, index - 128, index)
-        return np.where(2 * index == 128, 0, wave)
-
-    wave_y = signed((row // GZ)[:, None] + 16 * ((lane % CELLS) // 8)[None, :])
-    wave_z = signed((row % GZ)[:, None] + 16 * (lane % 8)[None, :])
-    waves = np.stack([wave_y, wave_z]).astype(np.float32)
-    return (*halves(lines), *halves(outer), *halves(inner), *halves(inner.T.copy()), twiddle, waves)
+        wave = jnp.where(2 * index > 128, index - 128, index)
+        return jnp.where(2 * index == 128, 0, wave).astype(F32)
+
+    return signed(row // GZ + 16 * (lane // 8)), signed(lax.rem(row, GZ) + 16 * lax.rem(lane, 8))
 
 
 def split(value):
@@ -73,50 +81,44 @@
     return lax.dot_general(left, right, (dims, ((), ())), preferred_element_type=F32)
 
 
-def greet_all():
+def shifted(a, b):
     gy, gz = lax.axis_index("gy"), lax.axis_index("gz")
-    barrier = pltpu.get_barrier_semaphore()
-
-    def greet(step, carry):
-        pl.semaphore_signal(barrier, inc=1, device_id=(lax.rem(gy + step, GY), gz), device_id_type=MESH)
-        pl.semaphore_signal(barrier, inc=1, device_id=(gy, lax.rem(gz + step, GZ)), device_id_type=MESH)
-        return carry
-
-    lax.fori_loop(1, 16, greet, 0)
-
-
-def meet_all(ready):
-    gy, gz = lax.axis_index("gy"), lax.axis_index("gz")
-    pl.semaphore_wait(pltpu.get_barrier_semaphore(), GY + GZ - 2)
-
-    def confirm(step, carry):
-        pl.semaphore_signal(ready, inc=1, device_id=(gy, lax.rem(gz + step, GZ)), device_id_type=MESH)
-        return carry
-
-    lax.fori_loop(1, GZ, confirm, 0)
-    pl.semaphore_wait(ready, GZ - 1)
+    return (lax.rem(gy + a + GY, GY), lax.rem(gz + b + GZ, GZ))
+
+
+def tell(sem, reach):
+    for a, b in neighbours():
+        pl.semaphore_signal(sem, inc=1, device_id=shifted(reach * a, reach * b), device_id_type=MESH)
 
 
 def exchange(source, target, send_sem, recv_sem, own_sem):
     gy, gz = lax.axis_index("gy"), lax.axis_index("gz")
     me = gy * GZ + gz
-
-    def send(step, carry):
-        ty, tz = lax.rem(gy + lax.rem(step, GY), GY), lax.rem(gz + step // GY, GZ)
-        pltpu.make_async_remote_copy(
-            source.at[ty * GZ + tz],
-            target.at[me],
-            send_sem,
-            recv_sem,
-            device_id=(ty, tz),
-            device_id_type=MESH,
-        ).start()
-        return carry
-
-    lax.fori_loop(1, PEERS, send, 0)
     own = pltpu.make_async_copy(source.at[me], target.at[me], own_sem)
     own.start()
     own.wait()
+    z, y_low = gy // 2, lax.rem(gy, 2)
+    y_high, x, core = gz // 8, lax.rem(gz // 2, 4), lax.rem(gz, 2)
+    for far in FAR:
+
+        def send(step, carry):
+            ty = lax.rem(z + far, 8) * 2 + lax.rem(y_low + lax.rem(step, 2), 2)
+            tz = (
+                lax.rem(y_high + lax.rem(step // 2, 2), 2) * 8
+                + lax.rem(x + lax.rem(step // 4, 4), 4) * 2
+                + lax.rem(core + step // 16, 2)
+            )
+            pltpu.make_async_remote_copy(
+                source.at[ty * GZ + tz],
+                target.at[me],
+                send_sem,
+                recv_sem,
+                device_id=(ty, tz),
+                device_id_type=MESH,
+            ).start()
+            return carry
+
+        lax.fori_loop(0 if far else 1, 32, send, 0)
     others = pl.ds(0, PEERS - 1)
     pltpu.make_async_copy(source.at[others], target.at[others], recv_sem).wait()
     pltpu.make_async_copy(source.at[others], target.at[others], send_sem).wait()
@@ -155,23 +157,19 @@
     return pl.ds(5, 3) if sending else pl.ds(0, 3)
 
 
-def halo(edge, around, sems):
+def halo_copies(edge, around, sems):
     gy, gz = lax.axis_index("gy"), lax.axis_index("gz")
-    copies = []
-    for index, (a, b) in enumerate(neighbours()):
-        copies.append(
-            pltpu.make_async_remote_copy(
-                edge.at[span(a, True), span(b, True)],
-                around.at[span(a, False), span(b, False)],
-                sems.at[index],
-                sems.at[8 + index],
-                device_id=(lax.rem(gy + a + GY, GY), lax.rem(gz + b + GZ, GZ)),
-                device_id_type=MESH,
-            )
+    return {
+        (a, b): pltpu.make_async_remote_copy(
+            edge.at[span(a, True), span(b, True)],
+            around.at[span(a, False), span(b, False)],
+            sems.at[index],
+            sems.at[8 + index],
+            device_id=shifted(a, b),
+            device_id_type=MESH,
         )
-    for copy in copies:
-        copy.start()
-    return copies
+        for index, (a, b) in enumerate(neighbours())
+    }
 
 
 def taken(cells, y, rows):
@@ -183,8 +181,8 @@
         cells[y, t, rows, :] = value[:, 128 * t : 128 * (t + 1)]
 
 
-def prepare(velocity, first, second, cells, edge, first_matrix, second_rows, second_matrix):
-    def place(y, carry):
+def place(velocity, cells, edge):
+    def row(y, carry):
         for c in range(4):
             value = velocity[c, y] if c < 3 else jnp.zeros((8, NL), F32)
             for t in range(4):
@@ -192,47 +190,73 @@
         edge[y] = taken(cells, y + 3, pl.ds(12, 32)).astype(BF).reshape(8, 4, NL)
         return carry
 
-    lax.fori_loop(0, 8, place, 0)
+    lax.fori_loop(0, 8, row, 0, unroll=UNROLL_PLACE)
+
+
+def bands(first, first_pick, second, second_pick, bias, first_matrix, second_rows, second_matrix, bias_rows):
+    eye = lax.broadcasted_iota(jnp.int32, (HIDDEN, HIDDEN), 0) == lax.broadcasted_iota(
+        jnp.int32, (HIDDEN, HIDDEN), 1
+    )
+    column = jnp.sum(jnp.where(eye, bias[...], 0.0), axis=1, keepdims=True)
+    base = dot(first[...], first_pick[...])
     for z in range(12):
-        rows = first[...] if z == 0 else pltpu.roll(first[...], 4 * z, axis=1)
+        rows = base if z == 0 else pltpu.roll(base, 4 * z, axis=1)
         first_matrix[pl.ds(HIDDEN * z, HIDDEN), :] = rows.astype(BF)
-    for z in range(8):
-        rows = second[...] if z == 0 else pltpu.roll(second[...], HIDDEN * z, axis=1)
-        for t in range(5):
-            second_rows[t, pl.ds(z, 27, stride=8), :] = rows[:27, 128 * t : 128 * (t + 1)]
-    second_matrix[...] = jnp.concatenate([second_rows[t] for t in range(5)], axis=1)[:, : 36 * HIDDEN].astype(BF)
-
-
-def spread(around, cells, stacked):
-    for y in (*range(3), *range(WIDE - 3, WIDE)):
-        put(cells, y, pl.ds(0, 4 * WIDE), around[y].astype(F32).reshape(4 * WIDE, NL))
-
+        bias_rows[pl.ds(HIDDEN * z, HIDDEN), :] = jnp.broadcast_to(column, (HIDDEN, 128))
+    taps = dot(second[...], second_pick[...])
+    channel = lax.broadcasted_iota(jnp.int32, (9, 256), 0)
+    for a in range(3):
+        near = taps[:, 256 * a : 256 * (a + 1)]
+        slope = pltpu.roll(near, HIDDEN, axis=1) - pltpu.roll(near, 256 - HIDDEN, axis=1)
+        value = jnp.where(lax.rem(channel, 3) == 2, slope, near)
+        gap = jnp.zeros((9, 112), F32)
+        base = jnp.concatenate(
+            [value[:, :80], gap, value[:, 80:160], gap, value[:, 160:240], gap, gap[:, :64]], axis=1
+        )
+        for z in range(8):
+            rows = base if z == 0 else pltpu.roll(base, HIDDEN * z, axis=1)
+            for t in range(5):
+                second_rows[t, pl.ds(72 * a + z, 9, stride=8), :] = rows[:, 128 * t : 128 * (t + 1)]
+    second_matrix[...] = jnp.concatenate([second_rows[t, :216] for t in range(5)], axis=1)[
+        :, : 36 * HIDDEN
+    ].astype(BF)
+
+
+def stack(cells, stacked, low, high):
+    def row(y, carry):
+        value = taken(cells, y, pl.ds(0, 4 * WIDE))
+        at = y * SPAN
+        stacked[pl.ds(pl.multiple_of(at, 8), 56), :] = pltpu.roll(value, 1, axis=1)
+        stacked[pl.ds(pl.multiple_of(at + 56, 8), 56), :] = value
+        stacked[pl.ds(pl.multiple_of(at + 112, 8), 56), :] = pltpu.roll(value, NL - 1, axis=1)
+        return carry
+
+    lax.fori_loop(low, high, row, 0, unroll=UNROLL_STACK)
+
+
+def spread_middle(around, cells, stacked):
     def sides(y, carry):
         put(cells, y, pl.ds(0, 12), around[y, pl.ds(0, 3)].astype(F32).reshape(12, NL))
         put(cells, y, pl.ds(44, 12), around[y, pl.ds(11, 3)].astype(F32).reshape(12, NL))
         return carry
 
-    lax.fori_loop(3, 11, sides, 0)
-
-    def stack(y, carry):
-        row = taken(cells, y, pl.ds(0, 4 * WIDE))
-        at = y * SPAN
-        stacked[pl.ds(pl.multiple_of(at, 8), 56), :] = pltpu.roll(row, 1, axis=1)
-        stacked[pl.ds(pl.multiple_of(at + 56, 8), 56), :] = row
-        stacked[pl.ds(pl.multiple_of(at + 112, 8), 56), :] = pltpu.roll(row, NL - 1, axis=1)
-        return carry
-
-    lax.fori_loop(0, WIDE, stack, 0)
+    lax.fori_loop(3, 11, sides, 0, unroll=UNROLL_STACK)
+    stack(cells, stacked, 3, 11)
+    stacked[pl.ds(11 * SPAN, 8), :] = jnp.zeros((8, NL), F32)
+
+
+def spread_ends(around, cells, stacked):
+    for y in (*range(3), *range(WIDE - 3, WIDE)):
+        put(cells, y, pl.ds(0, 4 * WIDE), around[y].astype(F32).reshape(4 * WIDE, NL))
+    stack(cells, stacked, 0, 3)
+    stack(cells, stacked, WIDE - 3, WIDE)
     stacked[pl.ds(WIDE * SPAN, 8), :] = jnp.zeros((8, NL), F32)
 
 
-def correct(bias, stacked, first_matrix, second_matrix, learned):
-    learned[0] = jnp.zeros((72, NL), F32)
-    learned[1] = jnp.zeros((72, NL), F32)
-
+def correct(bias, stacked, first_matrix, second_matrix, learned, low, high, fresh):
     def layer(y, carry):
         source = stacked[pl.ds(pl.multiple_of(y * SPAN, 8), 512), :].astype(BF)
-        before = dot(first_matrix[...], source) + bias[...]
+        before = dot(first_matrix[...], source) + bias[:, :1]
         hidden = before * (0.5 + 0.5 * jnp.tanh(0.5 * before))
         wide = jnp.concatenate(
             [
@@ -243,12 +267,15 @@
             axis=0,
         )
         part = dot(second_matrix[...], wide)
-        learned[y + 2] = part[:72]
+        if fresh:
+            learned[y + 2] = part[:72]
+        else:
+            learned[y + 2] += part[:72]
         learned[y + 1] += part[72:144]
         learned[y] += part[144:]
         return carry
 
-    lax.fori_loop(0, 12, layer, 0)
+    lax.fori_loop(low, high, layer, 0, unroll=UNROLL_LAYER)
 
 
 def advance(velocity, forcing, cells, learned, stepped):
@@ -272,12 +299,12 @@
         far = [lines(y + 3, c, 1) for c in range(3)]
         near = [lines(y + 3, c, -1) for c in range(3)]
         for i in range(3):
-            first = here[i] * here[0] + learned[y + 3, pl.ds(8 * i, 8), :].astype(BF).astype(F32)
-            rows = pl.ds(24 + 8 * i, 8)
+            first = here[i] * here[0] + learned[y + 3, pl.ds(24 * i, 8), :].astype(BF).astype(F32)
+            rows = pl.ds(24 * i + 8, 8)
             second = (over[i] * over[1] + learned[y + 4, rows, :]) - (
                 under[i] * under[1] + learned[y + 2, rows, :]
             )
-            third = (far[i] * far[2] - near[i] * near[2]) + learned[y + 3, pl.ds(48 + 8 * i, 8), :]
+            third = (far[i] * far[2] - near[i] * near[2]) + learned[y + 3, pl.ds(24 * i + 16, 8), :]
             divergence = (
                 (ahead(first) - behind(first)) * half[0] + second * half[1] + third * half[2]
             )
@@ -295,67 +322,75 @@
     lax.fori_loop(0, 8, move, 0)
 
 
-def first_rows(kernel):
-    rows = jnp.transpose(kernel, (0, 2, 4, 3, 1)).astype(F32)
-    rows = jnp.pad(rows, ((0, 0), (0, 0), (0, 0), (0, WIDE - 3), (0, 1)))
-    return jnp.pad(rows.reshape(HIDDEN, 9 * 4 * WIDE), ((0, 0), (0, 8)))
-
-
-def second_rows_of(kernel):
-    taps = kernel.astype(F32).reshape(3, 3, HIDDEN, 3, 3, 3)
-    taps = jnp.transpose(taps, (3, 1, 0, 5, 4, 2))
-    quiet = ((0, 0),) * 4
-    middle = jnp.pad(taps[:, :2], (*quiet, (1, 1), (0, 0)))
-    slope = jnp.pad(taps[:, 2:], (*quiet, (2, 0), (0, 0))) - jnp.pad(taps[:, 2:], (*quiet, (0, 2), (0, 0)))
-    rows = jnp.concatenate([middle, slope], axis=1)
-    rows = jnp.pad(rows, (*quiet, (0, 7), (0, 0))).reshape(27, 36 * HIDDEN)
-    return jnp.pad(rows, ((0, 5), (0, 4 * HIDDEN)))
+def picks():
+    first = np.zeros((81, 512))
+    second = np.zeros((27 * HIDDEN, 3 * 256))
+    for a in range(3):
+        for b in range(3):
+            for e in range(3):
+                for c in range(3):
+                    first[c * 27 + a * 9 + b * 3 + e, (3 * a + e) * 4 * WIDE + 4 * b + c] = 1.0
+                for c in range(HIDDEN):
+                    row = c * 27 + a * 9 + b * 3 + e
+                    lane = 80 * e + c
+                    second[row, 256 * a + lane + HIDDEN * (b + 1)] = 1.0
+    return first.astype(BF), second.astype(BF)
 
 
 def whole(
     velocity,
-    forcing,
     first,
+    first_pick,
     bias,
     second,
-    lines_high,
-    lines_low,
-    outer_high,
-    outer_low,
-    inner_high,
-    inner_low,
-    back_high,
-    back_low,
-    twiddle,
-    waves,
-    result,
-    cells,
-    edge,
-    around,
-    stacked,
-    first_matrix,
-    second_rows,
-    second_matrix,
-    learned,
-    stepped,
-    staged,
-    outgoing,
-    incoming,
-    outgoing_back,
-    incoming_back,
-    halo_sems,
-    sems,
-    ready,
+    second_pick,
+    forcing_far,
+    *rest,
 ):
-    greet_all()
-    prepare(velocity, first, second, cells, edge, first_matrix, second_rows, second_matrix)
-    meet_all(ready)
-    copies = halo(edge, around, halo_sems)
-    for copy in copies:
-        copy.wait()
-    spread(around, cells, stacked)
-    correct(bias, stacked, first_matrix, second_matrix, learned)
+    (
+        far_tables,
+        (result, cells, edge, around, stacked, first_matrix, second_rows, second_matrix, bias_rows, learned, stepped),
+        (staged, outgoing, incoming, outgoing_back, incoming_back),
+        (forcing, *tables),
+        (halo_sems, load_sems, sems, ready),
+    ) = [rest[slice(*bounds)] for bounds in ((0, 9), (9, 20), (20, 25), (25, 35), (35, 39))]
+    barrier = pltpu.get_barrier_semaphore()
+    tell(barrier, 1)
+    loads = [
+        pltpu.make_async_copy(source, target, load_sems.at[index])
+        for index, (source, target) in enumerate(zip((forcing_far, *far_tables), (forcing, *tables)))
+    ]
+    for load in loads:
+        load.start()
+    place(velocity, cells, edge)
+    pl.semaphore_wait(barrier, 8)
+    copies = halo_copies(edge, around, halo_sems)
+    for copy in copies.values():
+        copy.start()
+    tell(ready.at[0], 1)
+    learned[pl.ds(0, 5)] = jnp.zeros((5, 72, NL), F32)
+    bands(first, first_pick, second, second_pick, bias, first_matrix, second_rows, second_matrix, bias_rows)
+    copies[0, -1].wait_recv()
+    copies[0, 1].wait_recv()
+    pl.semaphore_wait(ready.at[0], 8)
+    tell(ready.at[1], 2)
+    spread_middle(around, cells, stacked)
+    correct(bias_rows, stacked, first_matrix, second_matrix, learned, 3, 9, True)
+    for (a, _), copy in copies.items():
+        if a != 0:
+            copy.wait_recv()
+    pl.semaphore_wait(ready.at[1], 8)
+    tell(ready.at[2], 4)
+    spread_ends(around, cells, stacked)
+    correct(bias_rows, stacked, first_matrix, second_matrix, learned, 9, 12, True)
+    correct(bias_rows, stacked, first_matrix, second_matrix, learned, 0, 3, False)
+    for load in loads:
+        load.wait()
     advance(velocity, forcing, cells, learned, stepped)
+    pl.semaphore_wait(ready.at[2], 8)
+    for copy in copies.values():
+        copy.wait_send()
+    lines_high, lines_low, outer_high, outer_low, inner_high, inner_low, back_high, back_low, twiddle = tables
     gy, gz = lax.axis_index("gy"), lax.axis_index("gz")
     nt = ((1,), (1,))
     high, low = split(stepped[...].reshape(3 * CELLS, NL))
@@ -388,7 +423,7 @@
     modes = dot(high, inner_high[...]) + (dot(low, inner_high[...]) + dot(high, inner_low[...]))
     slot = gy * GZ + gz
     wave_x = slot.astype(F32)
-    wave_y, wave_z = waves[0], waves[1]
+    wave_y, wave_z = signed_waves()
     squared = wave_x * wave_x + wave_y * wave_y + wave_z * wave_z
     inverse = jnp.where(squared > 0, 1.0 / jnp.maximum(squared, 1.0), 0.0)
     parts = [modes[PEERS * c : PEERS * (c + 1)] for c in range(3)]
@@ -426,33 +461,46 @@
 
 def body(velocity, forcing, first_kernel, first_bias, second_kernel):
     tables = spectral_tables()
-    vmem = pl.BlockSpec(memory_space=pltpu.VMEM)
-    bias = jnp.broadcast_to(first_bias[None, :], (12, HIDDEN)).reshape(12 * HIDDEN, 1)
+    first_pick, second_pick = picks()
+    vmem, away = pl.BlockSpec(memory_space=pltpu.VMEM), pl.BlockSpec(memory_space=pl.ANY)
     field = pl.pallas_call(
         whole,
         out_shape=jax.ShapeDtypeStruct((3, CELLS, NL), F32),
-        in_specs=[vmem] * (5 + len(tables)),
+        in_specs=[vmem] * 6 + [away] * (1 + len(tables)),
         out_specs=vmem,
         scratch_shapes=[
-            pltpu.VMEM((WIDE, 4, 4 * WIDE, 128), F32),
+            pltpu.VMEM((WIDE, 4, 64, 128), F32),
             pltpu.VMEM((8, 8, 4, NL), BF),
             pltpu.VMEM((WIDE, WIDE, 4, NL), BF),
             pltpu.VMEM((WIDE * SPAN + 8, NL), F32),
             pltpu.VMEM((12 * HIDDEN, 512), BF),
-            pltpu.VMEM((5, 216, 128), F32),
+            pltpu.VMEM((5, 288, 128), F32),
             pltpu.VMEM((216, 36 * HIDDEN), BF),
+            pltpu.VMEM((12 * HIDDEN, 128), F32),
             pltpu.VMEM((WIDE, 72, NL), F32),
             pltpu.VMEM((3, CELLS, NL), F32),
             pltpu.VMEM((4 * PEERS, 128), F32),
             *[pltpu.VMEM((PEERS, 4, 128), BF)] * 4,
+            pltpu.VMEM(forcing.shape, F32),
+            *[pltpu.VMEM(table.shape, table.dtype) for table in tables],
             pltpu.SemaphoreType.DMA((16,)),
+            pltpu.SemaphoreType.DMA((1 + len(tables),)),
             pltpu.SemaphoreType.DMA((6,)),
-            pltpu.SemaphoreType.REGULAR,
+            pltpu.SemaphoreType.REGULAR((3,)),
         ],
         compiler_params=pltpu.CompilerParams(
-            collective_id=0, has_side_effects=True, vmem_limit_bytes=56 * 2**20
+            collective_id=0, has_side_effects=True, vmem_limit_bytes=67_000_000
         ),
-    )(velocity, forcing, first_rows(first_kernel), bias, second_rows_of(second_kernel), *tables)
+    )(
+        velocity,
+        first_kernel.reshape(HIDDEN, 81),
+        first_pick,
+        first_bias.reshape(1, HIDDEN),
+        second_kernel.reshape(9, 27 * HIDDEN),
+        second_pick,
+        forcing,
+        *tables,
+    )
     return field.reshape(velocity.shape)
 
 

time: 69.3 us -> 62.8 us (0.906)
  Pallas kernels: 63.6 us -> 57.4 us
  other arithmetic: 0.71 us -> 0 us
    pallas_call x1, Pallas kernels: 63.6 us -> 57.4 us  [body(): pl.pallas_call(whole, out_shape=jax.ShapeDtypeStruct((3, CELLS, NL), F32)...]
    reshape x3 -> x4, local copies, waits for them, and re-layouts: 1.09 us -> 2.24 us  [the longest x2 1.43 us: body(): first_kernel.reshape(HIDDEN, 81)]
    unnamed x6 -> x2, local copies, waits for them, and re-layouts: 1.92 us -> 2.96 us
    transpose x1 -> x0, local copies, waits for them, and re-layouts: 0.92 us -> none  [second_rows_of(): taps = jnp.transpose(taps, (3, 1, 0, 5, 4, 2))]
    pad x3 -> x0, local copies, waits for them, and re-layouts: 0.73 us -> none  [the longest x1 0.64 us: second_rows_of(): return jnp.pad(rows, ((0, 5), (0, 4 * HIDDEN)))]
where the time goes in v3:
time: 62.8 us; the launch traced here: 62.6 us
  Pallas kernels  57.4 us (91%)
  local copies, waits for them, and re-layouts  5.21 us (8%)
    pallas_call x1, Pallas kernels, body(): pl.pallas_call(whole, out_shape=jax.ShapeDtypeStruct((3, CELLS, NL), F32)...  57.4 us
    unnamed x2, local copies, waits for them, and re-layouts  2.96 us
    reshape x2, local copies, waits for them, and re-layouts, body(): first_kernel.reshape(HIDDEN, 81)  1.43 us

profile of v3, /device:TPU:1, one launch (start us, length us, event | category | flops | bytes accessed | tf_op | source)
XLA Modules:
  0.0 62.6 jit_solution(1043117096523860746)
XLA Ops:
  0.0 0.8 %reshape.12 = bf16[16,81]{0,1:T(8,128)(2,1)S(1)} reshape(bf16[16,3,3,3,3]{0,4,3,2,1:T(4,128)(2,1)} %param.18) | data formatting | bytes 5184 | tf_op jit(solution)/shard_map/reshape | solution.py:496
  0.8 0.7 %copy.20.first = bf16[16,81]{1,0:T(8,128)(2,1)} copy(bf16[16,81]{0,1:T(8,128)(2,1)S(1)} %reshape.12) | data formatting | bytes 5184 | tf_op jit(solution)/shard_map/reshape | solution.py:496
  1.4 1.2 %copy.19 = bf16[9,16,3,3,3]{0,4,3,2,1:T(4,128)(2,1)S(1)} copy(bf16[9,16,3,3,3]{1,4,3,2,0:T(4,128)(2,1)} %param.20) | data formatting | bytes 15552 | tf_op args[4]
  2.6 0.1 reshape.14
  2.7 0.7 %copy.21.second = bf16[9,432]{1,0:T(8,128)(2,1)} copy(bf16[9,432]{0,1:T(8,128)(2,1)S(1)} %reshape.14) | data formatting | bytes 15552 | tf_op jit(solution)/shard_map/reshape | solution.py:499
  3.4 57.4 %shard_map.154 = f32[3,64,512]{2,1,0:T(8,128)} custom-call(f32[3,8,8,512]{3,2,1,0:T(8,128)} %velocity.1, bf16[16,81]{1,0:T(8,128)(2,1)} %copy.20.first, bf16[81,512]{1,0:T(8,128)(2,1)} %constant.22.clone.first_pick, f32[1,16]{1,0:T(1,128)} %bitcast.7, bf16[9,432]{1,0:T(8,128)(2,1)} %copy.21.second, bf16[432,768]{1,0:T(8,128)(2,1)} %constant.23.clone.second_pick, ...), custom_call_target="tpu_custom_call" | custom-call | tf_op jit(solution)/shard_map/pallas_call | solution.py:466
  60.8 1.8 %copy.23 = f32[3,8,8,512]{3,2,1,0:T(8,128)} copy(f32[3,8,8,512]{3,2,1,0:T(8,128)} %bitcast.6) | data formatting | bytes 786432
